TPU v7x, 32 devices: a whole 2x2x4 slice. The times are simulated.
32 devices in a mesh: face: 4 (over x, core), tile: 8 (over z, y).
Axes of the slice: x: 2, y: 2, z: 4, core: 2. Of those that a mesh axis runs over, the one named last changes fastest.
Arguments:
- pressure: float32 [64, 512, 256], P(None, ('face', 'tile')), may hold values from -0.8 to 0.8
- forcing: float32 [64, 512, 256], P(None, ('face', 'tile')), may hold values from -8 to 8
- stiffness: float32 [64, 512, 256], P(None, ('face', 'tile')), may hold values from 2 to 8
- vertical_op: float32 [64, 64], replicated, as said below
- col_inverse: float32 [4, 64, 64], replicated, as said below
Outputs:
- updated: float32 [64, 512, 256], P(None, ('face', 'tile'))
- new_residual: float32 [64, 512, 256], P(None, ('face', 'tile'))
Inputs may be any that keep to these rules, and one draw needn't show every extreme that they name: vertical_op is symmetric positive definite. col_inverse[l] is the float32 inverse of (0.02 + 16 / 4^l) I + vertical_op.
All inputs are finite; a program needn't handle non-finite values.
Results may differ from a plain program's by a relative error of at most 0.0003.
Values sent between devices are 32-bit elements; how exact they have to be, the bound alone decides.
No kernel may reach another device: no remote copies, remote signals or barrier semaphores. Data moves between devices by JAX's collectives and lax.ppermute only.
A program may use at most 128 MiB of HBM per device.

v0:
```python
import functools

import jax
import jax.numpy as jnp
from jax import lax
from jax.experimental import pallas as pl
from jax.experimental.pallas import tpu as pltpu
from jax.sharding import PartitionSpec as P

AXES = ("face", "tile")
LANES = 128
damping = 0.02
relax_weight = 0.6
nominal_stiff = 16.0
F32 = jnp.float32
BF16 = jnp.bfloat16


def nominal(level):
    return nominal_stiff / 4.0**level


def halves(x):
    hi = x.astype(BF16)
    return hi, (x - hi.astype(F32)).astype(BF16)


def column_matrix(m):
    hi = m.astype(BF16).astype(F32)
    lo = m - hi
    return jnp.concatenate([hi, hi, lo], axis=1).astype(BF16)


def column_apply(m3, t):
    z = m3.shape[0]
    out = []
    for i in range(t.shape[0] // z):
        hi, lo = halves(t[i * z : (i + 1) * z])
        out.append(
            jnp.dot(m3, jnp.concatenate([hi, lo, hi], axis=0), preferred_element_type=F32)
        )
    return out[0] if len(out) == 1 else jnp.concatenate(out, axis=0)


def lane_matrix(lanes_in, lanes_out, value, spread):
    i = lax.broadcasted_iota(jnp.int32, (lanes_in, lanes_out), 0)
    j = lax.broadcasted_iota(jnp.int32, (lanes_in, lanes_out), 1)
    hit = (j // 2 == i) if spread else (i // 2 == j)
    one = jnp.where(hit, F32(value), F32(0.0))
    return jnp.concatenate([one, one], axis=0).astype(BF16)


def lane_apply(v, m2):
    hi, lo = halves(v)
    return jnp.dot(jnp.concatenate([hi, lo], axis=1), m2, preferred_element_type=F32)


def side_rows(v, valid):
    lanes = v.shape[1]
    north = pltpu.roll(v, 1, 1)
    south = pltpu.roll(v, lanes - 1, 1)
    if valid == lanes:
        lane = lax.broadcasted_iota(jnp.int32, v.shape, 1)
        north = jnp.where(lane == 0, 0.0, north)
        south = jnp.where(lane == lanes - 1, 0.0, south)
    return north + south


def lap(west, mid, east, valid):
    return 4.0 * mid - (west + east) - side_rows(mid, valid)


def scaling(k, level):
    return (relax_weight * (damping + nominal(level))) / (damping + 4.0 * k)


def packed(blocks, valid):
    out = blocks[0]
    for i, v in enumerate(blocks[1:], 1):
        out = out + pltpu.roll(v, i * valid, 1)
    return out


def unpacked(v, i, valid):
    v = v if i == 0 else pltpu.roll(v, LANES - i * valid, 1)
    lane = lax.broadcasted_iota(jnp.int32, v.shape, 1)
    return jnp.where(lane < valid, v, 0.0)


def over(lo, hi, unroll, body):
    full = (hi - lo) // unroll
    if full > 1:
        lax.fori_loop(0, full, lambda i, _: (body(lo + i * unroll, unroll), 0)[1], 0)
    elif full == 1:
        body(lo, unroll)
    if (hi - lo) % unroll:
        body(lo + full * unroll, (hi - lo) % unroll)


class Field:
    def __init__(self, ref, z, halo):
        self.ref, self.z, self.halo = ref, z, halo

    def at(self, pos, n=1):
        start = (pos + self.halo) * self.z
        if not isinstance(start, int):
            start = pl.multiple_of(start, self.z)
        return pl.ds(start, n * self.z)

    def get(self, pos, n=1):
        return self.ref[self.at(pos, n), :]

    def put(self, pos, v, n=1):
        self.ref[self.at(pos, n), :] = v


def operator_part(r, d, k, s, level, valid, pos, n):
    rv, mid = r.get(pos, n), d.get(pos, n)
    sides = lap(d.get(pos - 1, n), mid, d.get(pos + 1, n), valid)
    return rv - (s.get(pos, n) * rv + k.get(pos, n) * sides - nominal(level) * mid)


def sweep(r, d, nxt, k, s, m3, level, valid, lo, hi, unroll):
    def body(pos, n):
        rv = operator_part(r, d, k, s, level, valid, pos, n)
        r.put(pos, rv, n)
        nxt.put(pos, column_apply(m3, s.get(pos, n) * rv), n)

    over(lo, hi, unroll, body)


def residue(r, d, k, s, level, valid, lo, hi, unroll):
    def body(pos, n):
        r.put(pos, operator_part(r, d, k, s, level, valid, pos, n), n)

    over(lo, hi, unroll, body)


def coarsen(fine, coarse, matrix, lo, hi):
    for pos in range(lo, hi):
        coarse.put(pos, lane_apply(fine.get(2 * pos) + fine.get(2 * pos + 1), matrix))


def refine(e, v3, spread, d, g, lo, hi):
    for pos in range(lo, hi):
        ev = e.get(pos)
        dv = lane_apply(ev, spread)
        gv = lane_apply(damping * ev + column_apply(v3, ev), spread)
        for i in (0, 1):
            d.put(2 * pos + i, dv)
            g.put(2 * pos + i, gv)


def after_coarse(r, d, g, nxt, k, s, m3, valid, lo, hi, unroll):
    def body(pos, n):
        sides = lap(d.get(pos - 1, n), d.get(pos, n), d.get(pos + 1, n), valid)
        rv = r.get(pos, n) - (k.get(pos, n) * sides + g.get(pos, n))
        r.put(pos, rv, n)
        nxt.put(pos, column_apply(m3, s.get(pos, n) * rv), n)

    over(lo, hi, unroll, body)


VM = pl.BlockSpec(memory_space=pltpu.VMEM)
ANY = pl.BlockSpec(memory_space=pl.ANY)


def lane_halves(ref, buf, sems, inward):
    out = []
    for i in range(2):
        far, near = ref.at[:, pl.ds(i * LANES, LANES)], buf.at[i]
        src, dst = (far, near) if inward else (near, far)
        out.append(pltpu.make_async_copy(src, dst, sems.at[i]))
    return out


def block_rows(buf, pos, z, n):
    rows = pl.ds(pos, z, stride=n)
    return jnp.concatenate([buf[0, rows, :], buf[1, rows, :]], axis=1)


def put_block_rows(buf, pos, z, n, v):
    rows = pl.ds(pos, z, stride=n)
    for i in range(2):
        buf[i, rows, :] = v[:, i * LANES : (i + 1) * LANES]


def kernel_call(fn, outs, scratch, args, aliases=None, far_in=0, far_out=0, sems=()):
    return pl.pallas_call(
        fn,
        out_shape=[jax.ShapeDtypeStruct(o, F32) for o in outs],
        in_specs=[ANY] * far_in + [VM] * (len(args) - far_in),
        out_specs=[VM] * (len(outs) - far_out) + [ANY] * far_out,
        scratch_shapes=[pltpu.VMEM(s, F32) for s in scratch]
        + [pltpu.SemaphoreType.DMA((n,)) for n in sems],
        input_output_aliases=aliases or {},
        name=fn.__name__,
        compiler_params=pltpu.CompilerParams(vmem_limit_bytes=40 * 1024 * 1024),
    )(*args)


def body(devices, pressure, forcing, stiffness, vertical_op, col_inverse):
    z, n0, r0 = pressure.shape
    pos = [n0 >> lev for lev in range(4)]
    valid = [r0 >> lev for lev in range(4)]
    lanes = [max(LANES, v) for v in valid]
    n1, n2, n3 = pos[1:]
    halo = [2, 4, 4, 5]
    span = [(pos[lev] + 2 * halo[lev]) * z for lev in range(4)]
    ext = [(span[lev], lanes[lev]) for lev in range(4)]
    own = [(pos[lev] * z, lanes[lev]) for lev in range(4)]

    def right(v, d=1):
        return lax.ppermute(v, AXES, [(i, (i + d) % devices) for i in range(devices)])

    def left(v, d=1):
        return lax.ppermute(v, AXES, [(i, (i - d) % devices) for i in range(devices)])

    flat = [v.reshape(z * n0, r0) for v in (pressure, forcing, stiffness)]

    def edges_of(i):
        return jnp.concatenate([pressure[:, i, :], stiffness[:, i, :]], axis=0)

    first, last = edges_of(0), edges_of(n0 - 1)
    pk_from_right, pk_from_left = left(first), right(last)

    def start_kernel(
        p, f, k, v, c, ke, se, re, de, to_left, to_right, pb, kbuf, pbuf, fbuf, ksem, psem, fsem
    ):
        copies = [
            lane_halves(far, buf, sem, True)
            for far, buf, sem in ((k, kbuf, ksem), (p, pbuf, psem), (f, fbuf, fsem))
        ]
        for pair in copies:
            for copy in pair:
                copy.start()
        ke, se, re, de = (Field(x, z, halo[0]) for x in (ke, se, re, de))
        pb = Field(pb, z, 1)
        m3 = column_matrix(c[0])
        v3 = column_matrix(v[...])
        pb.put(-1, jnp.zeros((z, r0), F32))
        pb.put(n0, jnp.zeros((z, r0), F32))

        for pair in copies[:2]:
            for copy in pair:
                copy.wait()

        def load(i, n):
            for j in range(n):
                kv = block_rows(kbuf, i + j, z, n0)
                ke.put(i + j, kv)
                se.put(i + j, scaling(kv, 0))
                pb.put(i + j, block_rows(pbuf, i + j, z, n0))

        over(0, n0, 4, load)

        for copy in copies[2]:
            copy.wait()

        def start(i, n):
            for j in range(n):
                q = i + j
                mid = pb.get(q)
                sides = lap(pb.get(q - 1), mid, pb.get(q + 1), valid[0])
                rv = block_rows(fbuf, q, z, n0) - (
                    damping * mid + ke.get(q) * sides + column_apply(v3, mid)
                )
                re.put(q, rv)
                de.put(q, column_apply(m3, se.get(q) * rv))

        over(0, n0, 4, start)
        for out, q, step in ((to_left, 0, 1), (to_right, n0 - 1, -1)):
            out[:z, :] = re.get(q)
            out[z:, :] = de.get(q + step)

    k_ext, s_ext, r_ext, d_ext, rd_left, rd_right = kernel_call(
        start_kernel,
        [ext[0]] * 4 + [(2 * z, r0)] * 2,
        [((n0 + 2) * z, r0)] + [(2, z * n0, LANES)] * 3,
        [*flat, vertical_op, col_inverse],
        far_in=3,
        sems=(2, 2, 2),
    )
    rd_from_right, rd_from_left = left(rd_left), right(rd_right)

    def stiff_kernel(ke, k1, k2, k3, to_left, to_right):
        ke = Field(ke, z, halo[0])
        ks = [ke] + [Field(x, z, 0) for x in (k1, k2, k3)]
        for lev in range(3):
            matrix = lane_matrix(lanes[lev], lanes[lev + 1], 1.0 / 16.0, False)
            coarsen(ks[lev], ks[lev + 1], matrix, 0, pos[lev + 1])
        for out, at in ((to_left, lambda i, n: i), (to_right, lambda i, n: n - 1 - i)):
            out = Field(out, z, 0)
            k01 = ke.get(at(1, n0))
            out.put(0, k01[:, :LANES])
            out.put(1, k01[:, LANES:])
            for i in range(3):
                out.put(2 + i, ks[1].get(at(i, n1)))
            for i in range(2):
                out.put(5 + i, packed([ks[2].get(2 * i + j) for j in range(2)], valid[2]))

    k1, k2, k3, ks_left, ks_right = kernel_call(
        stiff_kernel, own[1:] + [(7 * z, LANES)] * 2, [], [k_ext]
    )
    ks_from_right, ks_from_left = left(ks_left), right(ks_right)

    def fine_kernel(
        first, last, pk_l, pk_r, rd_l, rd_r, k1, c, ke_i, se_i, re_i, de_i,
        ke, se, re, de, c0, b1, d1, to_left, to_right, r_left, r_right, d2
    ):
        ke, se, re, de, d2 = (Field(x, z, halo[0]) for x in (ke, se, re, de, d2))
        m3 = column_matrix(c[0])
        for mine, pk, rd, q, step in (
            (first, pk_l, rd_l, 0, -1),
            (last, pk_r, rd_r, n0 - 1, 1),
        ):
            h = q + step
            kh = pk[z:, :]
            ke.put(h, kh)
            se.put(h, scaling(kh, 0))
            re.put(h, rd[:z, :] + kh * mine[:z, :])
            re.put(q, re.get(q) + ke.get(q) * pk[:z, :])
            for at in (h, q):
                de.put(at, column_apply(m3, se.get(at) * re.get(at)))
            de.put(h + step, rd[z:, :])
        sweep(re, de, d2, ke, se, m3, 0, valid[0], -1, n0 + 1, 3)
        residue(re, d2, ke, se, 0, valid[0], 0, n0, 2)
        c0 = Field(c0, z, 0)
        over(0, n0, 4, lambda i, n: c0.put(i, de.get(i, n) + d2.get(i, n), n))
        b1 = Field(b1, z, halo[1])
        coarsen(re, b1, lane_matrix(lanes[0], lanes[1], 0.25, False), 0, n1)
        d1 = Field(d1, z, halo[1])
        k1 = Field(k1, z, 0)
        m1 = column_matrix(c[1])
        for i in range(n1):
            d1.put(i, column_apply(m1, scaling(k1.get(i), 1) * b1.get(i)))
        for out, q, step in ((to_left, 0, 1), (to_right, n1 - 1, -1)):
            out[:z, :] = b1.get(q)
            out[z:, :] = d1.get(q + step)
        for out, q, step in ((r_left, 0, 1), (r_right, n0 - 1, -1)):
            out[:z, :] = re.get(q)
            out[z:, :] = re.get(q + step)

    k_ext, s_ext, r_ext, d_ext, c0, b1, d1, bd_left, bd_right, r_left, r_right = kernel_call(
        fine_kernel,
        [ext[0]] * 4 + [own[0], ext[1], ext[1]] + [(2 * z, lanes[1])] * 2 + [(2 * z, r0)] * 2,
        [ext[0]],
        [first, last, pk_from_left, pk_from_right, rd_from_left, rd_from_right, k1, col_inverse,
         k_ext, s_ext, r_ext, d_ext],
        {8: 0, 9: 1, 10: 2, 11: 3},
    )
    bd_from_right, bd_from_left = left(bd_left), right(bd_right)
    r_from_right, r_from_left = left(r_left), right(r_right)

    def second_kernel(
        bd_l, bd_r, ks_l, ks_r, k1_i, k2_i, c, b1_i, d1_i,
        b1, d1, k1, s1, b2, to_left, to_right, m_left, m_right, d2
    ):
        b1, d1, k1, s1, d2 = (Field(x, z, halo[1]) for x in (b1, d1, k1, s1, d2))
        b2 = Field(b2, z, halo[2])
        k1_i = Field(k1_i, z, 0)
        m3 = column_matrix(c[1])
        k1.put(0, k1_i.get(0, n1), n1)
        for ks, bd, q, step in ((ks_l, bd_l, -1, -1), (ks_r, bd_r, n1, 1)):
            ks = Field(ks, z, 0)
            for i in range(3):
                k1.put(q + i * step, ks.get(2 + i))
            b1.put(q, bd[:z, :])
            d1.put(q + step, bd[z:, :])
        over(-3, n1 + 3, 7, lambda i, n: s1.put(i, scaling(k1.get(i, n), 1), n))
        for q in (-1, n1):
            d1.put(q, column_apply(m3, s1.get(q) * b1.get(q)))
        sweep(b1, d1, d2, k1, s1, m3, 1, valid[1], -1, n1 + 1, 5)
        residue(b1, d2, k1, s1, 1, valid[1], 0, n1, 4)
        coarsen(b1, b2, lane_matrix(lanes[1], lanes[2], 0.25, False), 0, n2)
        for i in range(2):
            both = packed([b2.get(2 * i + j) for j in range(2)], valid[2])
            for out in (to_left, to_right):
                out[i * z : (i + 1) * z, :] = both
        for out, q, step in ((m_left, 0, 1), (m_right, n1 - 1, -1)):
            out = Field(out, z, 0)
            for i in range(3):
                out.put(i, b1.get(q + i * step))
            out.put(3, d2.get(q + step))
        d1.put(-1, d1.get(-1, n1 + 2) + d2.get(-1, n1 + 2), n1 + 2)

    r1, c1, k1e, s1e, b2, b2_left, b2_right, m_left, m_right = kernel_call(
        second_kernel,
        [ext[1]] * 4 + [ext[2]] + [(n2 // 2 * z, LANES)] * 2 + [(4 * z, LANES)] * 2,
        [ext[1]],
        [bd_from_left, bd_from_right, ks_from_left, ks_from_right, k1, k2, col_inverse, b1, d1],
        {7: 0, 8: 1},
    )
    b2_from_right, b2_from_left = left(b2_left), right(b2_right)
    m_from_right, m_from_left = left(m_left), right(m_right)

    def third_kernel(
        b2_l, b2_r, ks_l, ks_r, k2_i, c, b2_i, b2, d1, k2, s2, w3, to_left, to_right, d2
    ):
        b2, d1, k2, s2, d2 = (Field(x, z, halo[2]) for x in (b2, d1, k2, s2, d2))
        k2_i = Field(k2_i, z, 0)
        m3 = column_matrix(c[2])
        k2.put(0, k2_i.get(0, n2), n2)
        for ks, b, base in ((ks_l, b2_l, -n2), (ks_r, b2_r, n2)):
            ks, b = Field(ks, z, 0), Field(b, z, 0)
            for i in range(n2):
                b2.put(base + i, unpacked(b.get(i // 2), i % 2, valid[2]))
                k2.put(base + i, unpacked(ks.get(5 + i // 2), i % 2, valid[2]))
        for i in range(-n2, 2 * n2):
            s2.put(i, scaling(k2.get(i), 2))
            d1.put(i, column_apply(m3, s2.get(i) * b2.get(i)))
        sweep(b2, d1, d2, k2, s2, m3, 2, valid[2], -3, n2 + 3, 5)
        residue(b2, d2, k2, s2, 2, valid[2], -2, n2 + 2, 4)
        w3 = Field(w3, z, 0)
        for src, to, value in ((b2, 0, 0.25), (k2, 1, 1.0 / 16.0)):
            matrix = lane_matrix(lanes[2], lanes[3], value, False)
            rows = [
                lane_apply(src.get(2 * i) + src.get(2 * i + 1), matrix)
                for i in range(-1, n3 + 1)
            ]
            w3.put(to, packed(rows, valid[3]))
        for out, q in ((to_left, -2), (to_right, n2 + 1)):
            out = Field(out, z, 0)
            out.put(0, w3.get(0))
            out.put(1, w3.get(1))
            out.put(2, b2.get(q))
        d1.put(-2, d1.get(-2, n2 + 4) + d2.get(-2, n2 + 4), n2 + 4)

    r2, c2, k2e, s2e, w3, w_left, w_right = kernel_call(
        third_kernel,
        [ext[2]] * 4 + [(2 * z, LANES)] + [(3 * z, LANES)] * 2,
        [ext[2]],
        [b2_from_left, b2_from_right, ks_from_left, ks_from_right, k2, col_inverse, b2],
        {6: 0},
    )
    w_from_right, w_from_left = left(w_left, 2), right(w_right, 2)

    def coarse_kernel(w_l, w_r, w, c, v, c2, k2, s2, r2_i, r2, e2, b3, k3, s3, da, db, e3, d3, g3, d4, d5):
        b3, k3, s3, da, db, e3 = (Field(x, z, halo[3]) for x in (b3, k3, s3, da, db, e3))
        c2, k2, s2, r2, e2, d3, g3, d4, d5 = (
            Field(x, z, halo[2]) for x in (c2, k2, s2, r2, e2, d3, g3, d4, d5)
        )
        m3 = column_matrix(c[3])
        v3 = column_matrix(v[...])
        for src, base in ((w_l, -5), (w, -1), (w_r, 3)):
            src = Field(src, z, 0)
            bv, kv = src.get(0), src.get(1)
            for i in range(4):
                b3.put(base + i, unpacked(bv, i, valid[3]))
                k3.put(base + i, unpacked(kv, i, valid[3]))
        for i in range(-5, n3 + 5):
            s3.put(i, scaling(k3.get(i), 3))
            da.put(i, column_apply(m3, s3.get(i) * b3.get(i)))
        e3.put(-2, da.get(-2, n3 + 4), n3 + 4)
        for reach in (4, 3, 2):
            sweep(b3, da, db, k3, s3, m3, 3, valid[3], -reach, n3 + reach, 5)
            e3.put(-2, e3.get(-2, n3 + 4) + db.get(-2, n3 + 4), n3 + 4)
            da, db = db, da
        r2.put(-3, Field(w_l, z, 0).get(2))
        r2.put(n2 + 2, Field(w_r, z, 0).get(2))
        m2 = column_matrix(c[2])
        refine(e3, v3, lane_matrix(lanes[3], lanes[2], 1.0, True), d3, g3, -2, n3 + 2)
        after_coarse(r2, d3, g3, d4, k2, s2, m2, valid[2], -3, n2 + 3, 5)
        sweep(r2, d4, d5, k2, s2, m2, 2, valid[2], -2, n2 + 2, 4)
        q, m = -2, n2 + 4
        e2.put(q, c2.get(q, m) + d3.get(q, m) + d4.get(q, m) + d5.get(q, m), m)

    _, e2 = kernel_call(
        coarse_kernel,
        [ext[2]] * 2,
        [ext[3]] * 6 + [ext[2]] * 4,
        [w_from_left, w_from_right, w3, col_inverse, vertical_op, c2, k2e, s2e, r2],
        {8: 0},
    )

    def second_up_kernel(m_l, m_r, c, v, e2, k1, s1, c1, r1_i, r1, e1, d3, g3, d4, d5):
        e2 = Field(e2, z, halo[2])
        k1, s1, c1, r1, e1, d3, g3, d4, d5 = (
            Field(x, z, halo[1]) for x in (k1, s1, c1, r1, e1, d3, g3, d4, d5)
        )
        m1 = column_matrix(c[1])
        v3 = column_matrix(v[...])
        for m, q, step in ((m_l, -1, -1), (m_r, n1, 1)):
            m = Field(m, z, 0)
            for i in range(3):
                r1.put(q + i * step, m.get(i))
        refine(e2, v3, lane_matrix(lanes[2], lanes[1], 1.0, True), d3, g3, -2, n2 + 2)
        after_coarse(r1, d3, g3, d4, k1, s1, m1, valid[1], -3, n1 + 3, 7)
        sweep(r1, d4, d5, k1, s1, m1, 1, valid[1], -2, n1 + 2, 6)
        q, n = -2, n1 + 4
        e1.put(q, c1.get(q, n) + d3.get(q, n) + d4.get(q, n) + d5.get(q, n), n)
        for m, at in ((m_l, -2), (m_r, n1 + 1)):
            e1.put(at, e1.get(at) + Field(m, z, 0).get(3))

    _, e1 = kernel_call(
        second_up_kernel,
        [ext[1]] * 2,
        [ext[1]] * 4,
        [m_from_left, m_from_right, col_inverse, vertical_op, e2, k1e, s1e, c1, r1],
        {8: 0},
    )

    def last_kernel(
        p, r_l, r_r, ks_l, ks_r, c, v, e1, c0, ke_i, se_i, re_i,
        ke, se, re, up, res, d3, g3, d4, d5, pbuf, ubuf, vbuf, psem, usem, vsem
    ):
        loads = lane_halves(p, pbuf, psem, True)
        for copy in loads:
            copy.start()
        e1 = Field(e1, z, halo[1])
        ke, se, re, d4, d5 = (Field(x, z, halo[0]) for x in (ke, se, re, d4, d5))
        d3, g3 = (Field(x, z, 4) for x in (d3, g3))
        c0 = Field(c0, z, 0)
        m3 = column_matrix(c[0])
        v3 = column_matrix(v[...])
        for r, ks, q, step in ((r_l, ks_l, -1, -1), (r_r, ks_r, n0, 1)):
            re.put(q, r[:z, :])
            re.put(q + step, r[z:, :])
            ks = Field(ks, z, 0)
            kv = jnp.concatenate([ks.get(0), ks.get(1)], axis=1)
            ke.put(q + step, kv)
            se.put(q + step, scaling(kv, 0))
        refine(e1, v3, lane_matrix(lanes[1], lanes[0], 1.0, True), d3, g3, -2, n1 + 2)
        after_coarse(re, d3, g3, d4, ke, se, m3, valid[0], -2, n0 + 2, 4)
        sweep(re, d4, d5, ke, se, m3, 0, valid[0], -1, n0 + 1, 3)

        for copy in loads:
            copy.wait()

        def total(i, n):
            for j in range(n):
                q = i + j
                c = c0.get(q) + d3.get(q) + d4.get(q) + d5.get(q)
                put_block_rows(ubuf, q, z, n0, block_rows(pbuf, q, z, n0) + c)

        over(0, n0, 4, total)
        stores = lane_halves(up, ubuf, usem, False)
        for copy in stores:
            copy.start()

        def finish(i, n):
            for j in range(n):
                q = i + j
                rv = operator_part(re, d5, ke, se, 0, valid[0], q, 1)
                put_block_rows(vbuf, q, z, n0, rv)

        over(0, n0, 4, finish)
        more = lane_halves(res, vbuf, vsem, False)
        for copy in more:
            copy.start()
        for copy in stores + more:
            copy.wait()

    outs = kernel_call(
        last_kernel,
        [ext[0]] * 3 + [(z * n0, r0)] * 2,
        [((n0 + 8) * z, r0)] * 2 + [ext[0]] * 2 + [(2, z * n0, LANES)] * 3,
        [flat[0], r_from_left, r_from_right, ks_from_left, ks_from_right, col_inverse, vertical_op,
         e1, c0, k_ext, s_ext, r_ext],
        {9: 0, 10: 1, 11: 2},
        far_in=1,
        far_out=2,
        sems=(2, 2, 2),
    )
    return tuple(o.reshape(z, n0, r0) for o in outs[3:])


def solution(mesh):
    devices = 1
    for axis in AXES:
        devices *= mesh.shape[axis]
    split = P(None, AXES, None)
    return jax.shard_map(
        functools.partial(body, devices),
        mesh=mesh,
        in_specs=(split, split, split, P(), P()),
        out_specs=(split, split),
        check_vma=False,
    )
```

profile of v0, /device:TPU:0, one launch (start us, length us, event | category | flops | bytes accessed | tf_op | source)
XLA Modules:
  0.0 94.1 jit_solution(12196431459165659419)
XLA Ops:
  0.6 0.0 copy-start.2
  0.6 1.4 %fusion = (f32[64,1,256]{2,1,0:T(1,128)S(1)}, f32[64,1,256]{2,1,0:T(1,128)S(1)}) fusion(f32[64,16,256]{2,1,0:T(8,128)} %param.5), kind=kLoop, calls=%fused_computation.6 | loop fusion | bytes 262144 | tf_op jit(solution)/shard_map/slice | solution.py:222
  2.0 1.3 %fusion.1 = (f32[64,1,256]{2,1,0:T(1,128)S(1)}, f32[64,1,256]{2,1,0:T(1,128)S(1)}) fusion(f32[64,16,256]{2,1,0:T(8,128)} %param.7), kind=kLoop, calls=%fused_computation.7 | loop fusion | bytes 262144 | tf_op jit(solution)/shard_map/slice | solution.py:222
  3.4 6.5 %collective-permute-start.1 = (f32[128,256]{1,0:T(8,128)S(1)}, f32[128,256]{1,0:T(8,128)S(1)}, u32[]{:S(2)}, u32[]{:S(2)}) collective-permute-start(f32[128,256]{1,0:T(8,128)S(1)} %pad_maximum_fusion.first), channel_id=1, source_target_pairs={{0,31},{1,0},{2,1},{3,2},{4,3},{5,4},{6,5},{7,6},{8,7},{9,8},{10,9... | collective-permute-start | bytes 393224 | tf_op jit(solution)/shard_map/ppermute | solution.py:217
  9.8 0.0 copy-done.2
  9.8 0.0 copy-start
  9.8 0.9 copy-done
  10.7 0.0 copy-start.3
  10.7 1.2 %copy-done.3 = f32[64,16,256]{2,1,0:T(8,128)S(1)} copy-done((f32[64,16,256]{2,1,0:T(8,128)S(1)}, f32[64,16,256]{2,1,0:T(8,128)}, u32[]{:S(2)}) %copy-start.3) | copy-done | bytes 1048600
  11.9 0.0 copy-start.4
  11.9 1.2 %copy-done.4 = f32[64,16,256]{2,1,0:T(8,128)S(1)} copy-done((f32[64,16,256]{2,1,0:T(8,128)S(1)}, f32[64,16,256]{2,1,0:T(8,128)}, u32[]{:S(2)}) %copy-start.4) | copy-done | bytes 1048600
  13.2 0.0 copy-start.5
  13.2 0.8 copy-done.5
  13.9 3.3 %start_kernel.1 = (f32[1280,256]{1,0:T(8,128)S(1)}, f32[1280,256]{1,0:T(8,128)S(1)}, f32[1280,256]{1,0:T(8,128)S(1)}, f32[1280,256]{1,0:T(8,128)S(1)}, f32[128,256]{1,0:T(8,128)S(1)}, /*index=5*/f32[128,256]{1,0:T(8,128)S(1)}) custom-call(f32[1024,256]{1,0:T(8,128)S(1)} %bitcast.13, f32[1024,256]{1,0:T(8,128)S(1)} %bitcast.16, f32[1024,256]{1,0:T(8,128)S(1)} %bitcast.15, ...), custom_call_target="tpu_custom_call" | custom-call | tf_op jit(solution)/shard_map/start_kernel/pallas_call | solution.py:189
  17.3 0.0 copy-start.1
  17.3 1.2 %stiff_kernel.1 = (f32[512,128]{1,0:T(8,128)S(1)}, f32[256,128]{1,0:T(8,128)S(1)}, f32[128,128]{1,0:T(8,128)}, f32[448,128]{1,0:T(8,128)S(1)}, f32[448,128]{1,0:T(8,128)S(1)}) custom-call(f32[1280,256]{1,0:T(8,128)S(1)} %get-tuple-element.44.ke.ke_i), custom_call_target="tpu_custom_call" | custom-call | tf_op jit(solution)/shard_map/stiff_kernel/pallas_call | solution.py:189
  18.5 0.0 collective-permute-start.6
  18.5 5.3 %collective-permute-start.7 = (f32[448,128]{1,0:T(8,128)S(1)}, f32[448,128]{1,0:T(8,128)S(1)}, u32[]{:S(2)}, u32[]{:S(2)}) collective-permute-start(f32[448,128]{1,0:T(8,128)S(1)} %get-tuple-element.52), channel_id=1, source_target_pairs={{0,31},{1,0},{2,1},{3,2},{4,3},{5,4},{6,5},{7,6},{8,7},{9,8},{10,9... | collective-permute-start | bytes 688136 | tf_op jit(solution)/shard_map/ppermute | solution.py:217
  23.8 0.1 collective-permute-start
  23.9 0.1 collective-permute-start.2
  24.0 0.0 collective-permute-done.1.pk_r
  24.0 5.3 %collective-permute-start.3 = (f32[128,256]{1,0:T(8,128)S(1)}, f32[128,256]{1,0:T(8,128)S(1)}, u32[]{:S(2)}, u32[]{:S(2)}) collective-permute-start(f32[128,256]{1,0:T(8,128)S(1)} %get-tuple-element.43), channel_id=1, source_target_pairs={{0,31},{1,0},{2,1},{3,2},{4,3},{5,4},{6,5},{7,6},{8,7},{9,8},{10,9... | collective-permute-start | bytes 393224 | tf_op jit(solution)/shard_map/ppermute | solution.py:217
  29.3 4.5 %collective-permute-done.pk_l = f32[128,256]{1,0:T(8,128)S(1)} collective-permute-done((f32[128,256]{1,0:T(8,128)S(1)}, f32[128,256]{1,0:T(8,128)S(1)}, u32[]{:S(2)}, u32[]{:S(2)}) %collective-permute-start) | collective-permute-done | bytes 131104 | tf_op jit(solution)/shard_map/ppermute | solution.py:214
  33.8 2.7 %collective-permute-done.2.rd_l = f32[128,256]{1,0:T(8,128)S(1)} collective-permute-done((f32[128,256]{1,0:T(8,128)S(1)}, f32[128,256]{1,0:T(8,128)S(1)}, u32[]{:S(2)}, u32[]{:S(2)}) %collective-permute-start.2) | collective-permute-done | bytes 131104 | tf_op jit(solution)/shard_map/ppermute | solution.py:214
  36.5 2.5 %collective-permute-done.3.rd_r = f32[128,256]{1,0:T(8,128)S(1)} collective-permute-done((f32[128,256]{1,0:T(8,128)S(1)}, f32[128,256]{1,0:T(8,128)S(1)}, u32[]{:S(2)}, u32[]{:S(2)}) %collective-permute-start.3) | collective-permute-done | bytes 131104 | tf_op jit(solution)/shard_map/ppermute | solution.py:217
  39.1 0.0 copy-done.1
  39.1 4.2 %fine_kernel.1 = (f32[1280,256]{1,0:T(8,128)S(1)}, f32[1280,256]{1,0:T(8,128)S(1)}, f32[1280,256]{1,0:T(8,128)S(1)}, f32[1280,256]{1,0:T(8,128)S(1)}, f32[1024,2...) custom-call(f32[128,256]{1,0:T(8,128)S(1)} %pad_maximum_fusion.first, ...), custom_call_target="tpu_custom_call", output_to_operand_aliasing={{0}: (8, {}), {1}: (9, {}), {2}: (10, {}), {3}: (11, {})} | custom-call | tf_op jit(solution)/shard_map/fine_kernel/pallas_call | solution.py:189
  43.3 0.1 collective-permute-start.8
  43.4 5.3 %collective-permute-start.9 = (f32[128,128]{1,0:T(8,128)S(1)}, f32[128,128]{1,0:T(8,128)S(1)}, u32[]{:S(2)}, u32[]{:S(2)}) collective-permute-start(f32[128,128]{1,0:T(8,128)S(1)} %get-tuple-element.54), channel_id=1, source_target_pairs={{0,31},{1,0},{2,1},{3,2},{4,3},{5,4},{6,5},{7,6},{8,7},{9,8},{10,9... | collective-permute-start | bytes 196616 | tf_op jit(solution)/shard_map/ppermute | solution.py:217
  48.7 2.6 %collective-permute-done.8.bd_l = f32[128,128]{1,0:T(8,128)S(1)} collective-permute-done((f32[128,128]{1,0:T(8,128)S(1)}, f32[128,128]{1,0:T(8,128)S(1)}, u32[]{:S(2)}, u32[]{:S(2)}) %collective-permute-start.8) | collective-permute-done | bytes 65568 | tf_op jit(solution)/shard_map/ppermute | solution.py:214
  51.3 0.0 collective-permute-done.9.bd_r
  51.3 0.0 collective-permute-done.6.ks_l
  51.3 0.0 collective-permute-done.7.ks_r
  51.3 0.0 copy-start.6
  51.3 1.5 %second_kernel.1 = (f32[1024,128]{1,0:T(8,128)S(1)}, f32[1024,128]{1,0:T(8,128)S(1)}, f32[1024,128]{1,0:T(8,128)S(1)}, f32[1024,128]{1,0:T(8,128)S(1)}, f32[768,...) custom-call(f32[128,128]{1,0:T(8,128)S(1)} %collective-permute-done., ...), custom_call_target="tpu_custom_call", output_to_operand_aliasing={{0}: (7, {}), {1}: (8, {})} | custom-call | tf_op jit(solution)/shard_map/second_kernel/pallas_call | solution.py:189
  52.9 0.1 collective-permute-start.12
  52.9 5.3 %collective-permute-start.13 = (f32[128,128]{1,0:T(8,128)S(1)}, f32[128,128]{1,0:T(8,128)S(1)}, u32[]{:S(2)}, u32[]{:S(2)}) collective-permute-start(f32[128,128]{1,0:T(8,128)S(1)} %get-tuple-element.61), channel_id=1, source_target_pairs={{0,31},{1,0},{2,1},{3,2},{4,3},{5,4},{6,5},{7,6},{8,7},{9,8},{10,9... | collective-permute-start | bytes 196616 | tf_op jit(solution)/shard_map/ppermute | solution.py:217
  58.3 2.1 %collective-permute-done.12.b2_l = f32[128,128]{1,0:T(8,128)S(1)} collective-permute-done((f32[128,128]{1,0:T(8,128)S(1)}, f32[128,128]{1,0:T(8,128)S(1)}, u32[]{:S(2)}, u32[]{:S(2)}) %collective-permute-start.12) | collective-permute-done | bytes 65568 | tf_op jit(solution)/shard_map/ppermute | solution.py:214
  60.4 0.2 collective-permute-done.13.b2_r
  60.6 1.6 %third_kernel.1 = (f32[768,128]{1,0:T(8,128)S(1)}, f32[768,128]{1,0:T(8,128)S(1)}, f32[768,128]{1,0:T(8,128)S(1)}, f32[768,128]{1,0:T(8,128)S(1)}, f32[128,128]{...) custom-call(f32[128,128]{1,0:T(8,128)S(1)} %collective-permute-done.12.b2_l, ...), custom_call_target="tpu_custom_call", output_to_operand_aliasing={{0}: (6, {})} | custom-call | tf_op jit(solution)/shard_map/third_kernel/pallas_call | solution.py:189
  62.3 0.1 collective-permute-start.14
  62.3 0.1 collective-permute-start.10
  62.4 5.7 %collective-permute-start.11 = (f32[256,128]{1,0:T(8,128)S(1)}, f32[256,128]{1,0:T(8,128)S(1)}, u32[]{:S(2)}, u32[]{:S(2)}) collective-permute-start(f32[256,128]{1,0:T(8,128)S(1)} %get-tuple-element.59), channel_id=1, source_target_pairs={{0,31},{1,0},{2,1},{3,2},{4,3},{5,4},{6,5},{7,6},{8,7},{9,8},{10,9... | collective-permute-start | bytes 393224 | tf_op jit(solution)/shard_map/ppermute | solution.py:217
  68.1 0.0 collective-permute-start.4
  68.1 5.3 %collective-permute-start.5 = (f32[128,256]{1,0:T(8,128)S(1)}, f32[128,256]{1,0:T(8,128)S(1)}, u32[]{:S(2)}, u32[]{:S(2)}) collective-permute-start(f32[128,256]{1,0:T(8,128)S(1)} %get-tuple-element.50), channel_id=1, source_target_pairs={{0,31},{1,0},{2,1},{3,2},{4,3},{5,4},{6,5},{7,6},{8,7},{9,8},{10,9... | collective-permute-start | bytes 393224 | tf_op jit(solution)/shard_map/ppermute | solution.py:217
  73.5 0.0 collective-permute-done.14.w_l
  73.5 0.0 collective-permute-start.15
  73.5 4.6 %collective-permute-done.15.w_r = f32[192,128]{1,0:T(8,128)S(1)} collective-permute-done((f32[192,128]{1,0:T(8,128)S(1)}, f32[192,128]{1,0:T(8,128)S(1)}, u32[]{:S(2)}, u32[]{:S(2)}) %collective-permute-start.15) | collective-permute-done | bytes 98336 | tf_op jit(solution)/shard_map/ppermute | solution.py:217
  78.1 0.0 copy-done.6
  78.1 3.9 %coarse_kernel.1 = (f32[768,128]{1,0:T(8,128)S(1)}, f32[768,128]{1,0:T(8,128)S(1)}) custom-call(f32[192,128]{1,0:T(8,128)S(1)} %collective-permute-done.14.w_l, f32[192,128]{1,0:T(8,128)S(1)} %collective-permute-done.15.w_r, f32[128,128]{1,0:T(8,128)S(1)} %get-tuple-element.65.w, f32[4,64,64]{2,1,0:T(8,128)S(1)} %copy-done.1, ...), custom_call_target="tpu_custom_call", output_to_operand_aliasing={{0}: (8, {})} | custom-call | tf_op jit(solution)/shard_map/coarse_kernel/pallas_call | solution.py:189
  82.0 0.0 collective-permute-done.10.m_l
  82.0 0.0 collective-permute-done.11.m_r
  82.0 2.9 %second_up_kernel.1 = (f32[1024,128]{1,0:T(8,128)S(1)}, f32[1024,128]{1,0:T(8,128)S(1)}) custom-call(f32[256,128]{1,0:T(8,128)S(1)} %collective-permute-done.10.m_l, f32[256,128]{1,0:T(8,128)S(1)} %collective-permute-done.11.m_r, f32[4,64,64]{2,1,0:T(8,128)S(1)} %copy-done.1, f32[64,64]{1,0:T(8,128)S(1)} %copy-done.6, ...), custom_call_target="tpu_custom_call", output_to_operand_aliasing={{0}: (8, {})} | custom-call | tf_op jit(solution)/shard_map/second_up_kernel/pallas_call | solution.py:189
  84.9 0.0 collective-permute-done.4.r_l
  84.9 0.0 collective-permute-done.5.r_r
  85.0 9.2 %last_kernel.1 = (f32[1280,256]{1,0:T(8,128)S(1)}, f32[1280,256]{1,0:T(8,128)S(1)}, f32[1280,256]{1,0:T(8,128)S(1)}, f32[1024,256]{1,0:T(8,128)}, f32[1024,256]{1,0:T(8,128)}) custom-call(f32[1024,256]{1,0:T(8,128)S(1)} %bitcast.14, f32[128,256]{1,0:T(8,128)S(1)} %collective-permute-done.4.r_l, ...), custom_call_target="tpu_custom_call", output_to_operand_aliasing={{0}: (9, {}), {1}: (10, {}), {2}: (11, {})} | custom-call | tf_op jit(solution)/shard_map/last_kernel/pallas_call | solution.py:189
  (4 shorter events, 0.0 us)
Async XLA Ops:
  0.6 9.2 %copy-start.2 = (f32[64,16,256]{2,1,0:T(8,128)S(1)}, f32[64,16,256]{2,1,0:T(8,128)}, u32[]{:S(2)}) copy-start(f32[64,16,256]{2,1,0:T(8,128)} %param.5) | copy-start | bytes 3145732
  3.4 20.6 %collective-permute-start.1 = (f32[128,256]{1,0:T(8,128)S(1)}, f32[128,256]{1,0:T(8,128)S(1)}, u32[]{:S(2)}, u32[]{:S(2)}) collective-permute-start(f32[128,256]{1,0:T(8,128)S(1)} %pad_maximum_fusion.first), channel_id=1, source_target_pairs={{0,31},{1,0},{2,1},{3,2},{4,3},{5,4},{6,5},{7,6},{8,7},{9,8},{10,9... | collective-permute-start | bytes 393224 | tf_op jit(solution)/shard_map/ppermute | solution.py:217
  9.8 0.9 copy-start
  10.7 1.2 %copy-start.3 = (f32[64,16,256]{2,1,0:T(8,128)S(1)}, f32[64,16,256]{2,1,0:T(8,128)}, u32[]{:S(2)}) copy-start(f32[64,16,256]{2,1,0:T(8,128)} %param.7) | copy-start | bytes 3145732
  11.9 1.2 %copy-start.4 = (f32[64,16,256]{2,1,0:T(8,128)S(1)}, f32[64,16,256]{2,1,0:T(8,128)}, u32[]{:S(2)}) copy-start(f32[64,16,256]{2,1,0:T(8,128)} %param.6) | copy-start | bytes 3145732
  13.2 0.8 copy-start.5
  17.3 21.8 %copy-start.1 = (f32[4,64,64]{2,1,0:T(8,128)S(1)}, f32[4,64,64]{2,1,0:T(8,128)}, u32[]{:S(2)}) copy-start(f32[4,64,64]{2,1,0:T(8,128)} %c.13) | copy-start | bytes 196612
  18.5 32.8 %collective-permute-start.6 = (f32[448,128]{1,0:T(8,128)S(1)}, f32[448,128]{1,0:T(8,128)S(1)}, u32[]{:S(2)}, u32[]{:S(2)}) collective-permute-start(f32[448,128]{1,0:T(8,128)S(1)} %get-tuple-element.51), channel_id=1, source_target_pairs={{0,1},{1,2},{2,3},{3,4},{4,5},{5,6},{6,7},{7,8},{8,9},{9,10},{10,1... | collective-permute-start | bytes 688136 | tf_op jit(solution)/shard_map/ppermute | solution.py:214
  18.5 32.8 %collective-permute-start.7 = (f32[448,128]{1,0:T(8,128)S(1)}, f32[448,128]{1,0:T(8,128)S(1)}, u32[]{:S(2)}, u32[]{:S(2)}) collective-permute-start(f32[448,128]{1,0:T(8,128)S(1)} %get-tuple-element.52), channel_id=1, source_target_pairs={{0,31},{1,0},{2,1},{3,2},{4,3},{5,4},{6,5},{7,6},{8,7},{9,8},{10,9... | collective-permute-start | bytes 688136 | tf_op jit(solution)/shard_map/ppermute | solution.py:217
  23.8 10.0 %collective-permute-start = (f32[128,256]{1,0:T(8,128)S(1)}, f32[128,256]{1,0:T(8,128)S(1)}, u32[]{:S(2)}, u32[]{:S(2)}) collective-permute-start(f32[128,256]{1,0:T(8,128)S(1)} %pad_maximum_fusion.1.last), channel_id=1, source_target_pairs={{0,1},{1,2},{2,3},{3,4},{4,5},{5,6},{6,7},{7,8},{8,9},{9,10},{10,1... | collective-permute-start | bytes 393224 | tf_op jit(solution)/shard_map/ppermute | solution.py:214
  23.9 12.6 %collective-permute-start.2 = (f32[128,256]{1,0:T(8,128)S(1)}, f32[128,256]{1,0:T(8,128)S(1)}, u32[]{:S(2)}, u32[]{:S(2)}) collective-permute-start(f32[128,256]{1,0:T(8,128)S(1)} %get-tuple-element.42), channel_id=1, source_target_pairs={{0,1},{1,2},{2,3},{3,4},{4,5},{5,6},{6,7},{7,8},{8,9},{9,10},{10,1... | collective-permute-start | bytes 393224 | tf_op jit(solution)/shard_map/ppermute | solution.py:214
  24.0 15.1 %collective-permute-start.3 = (f32[128,256]{1,0:T(8,128)S(1)}, f32[128,256]{1,0:T(8,128)S(1)}, u32[]{:S(2)}, u32[]{:S(2)}) collective-permute-start(f32[128,256]{1,0:T(8,128)S(1)} %get-tuple-element.43), channel_id=1, source_target_pairs={{0,31},{1,0},{2,1},{3,2},{4,3},{5,4},{6,5},{7,6},{8,7},{9,8},{10,9... | collective-permute-start | bytes 393224 | tf_op jit(solution)/shard_map/ppermute | solution.py:217
  43.3 8.0 %collective-permute-start.8 = (f32[128,128]{1,0:T(8,128)S(1)}, f32[128,128]{1,0:T(8,128)S(1)}, u32[]{:S(2)}, u32[]{:S(2)}) collective-permute-start(f32[128,128]{1,0:T(8,128)S(1)} %get-tuple-element.53), channel_id=1, source_target_pairs={{0,1},{1,2},{2,3},{3,4},{4,5},{5,6},{6,7},{7,8},{8,9},{9,10},{10,1... | collective-permute-start | bytes 196616 | tf_op jit(solution)/shard_map/ppermute | solution.py:214
  43.4 7.9 %collective-permute-start.9 = (f32[128,128]{1,0:T(8,128)S(1)}, f32[128,128]{1,0:T(8,128)S(1)}, u32[]{:S(2)}, u32[]{:S(2)}) collective-permute-start(f32[128,128]{1,0:T(8,128)S(1)} %get-tuple-element.54), channel_id=1, source_target_pairs={{0,31},{1,0},{2,1},{3,2},{4,3},{5,4},{6,5},{7,6},{8,7},{9,8},{10,9... | collective-permute-start | bytes 196616 | tf_op jit(solution)/shard_map/ppermute | solution.py:217
  51.3 26.8 %copy-start.6 = (f32[64,64]{1,0:T(8,128)S(1)}, f32[64,64]{1,0:T(8,128)}, u32[]{:S(2)}) copy-start(f32[64,64]{1,0:T(8,128)} %v.7) | copy-start | bytes 49156
  52.9 7.5 %collective-permute-start.12 = (f32[128,128]{1,0:T(8,128)S(1)}, f32[128,128]{1,0:T(8,128)S(1)}, u32[]{:S(2)}, u32[]{:S(2)}) collective-permute-start(f32[128,128]{1,0:T(8,128)S(1)} %get-tuple-element.60), channel_id=1, source_target_pairs={{0,1},{1,2},{2,3},{3,4},{4,5},{5,6},{6,7},{7,8},{8,9},{9,10},{10,1... | collective-permute-start | bytes 196616 | tf_op jit(solution)/shard_map/ppermute | solution.py:214
  52.9 7.7 %collective-permute-start.13 = (f32[128,128]{1,0:T(8,128)S(1)}, f32[128,128]{1,0:T(8,128)S(1)}, u32[]{:S(2)}, u32[]{:S(2)}) collective-permute-start(f32[128,128]{1,0:T(8,128)S(1)} %get-tuple-element.61), channel_id=1, source_target_pairs={{0,31},{1,0},{2,1},{3,2},{4,3},{5,4},{6,5},{7,6},{8,7},{9,8},{10,9... | collective-permute-start | bytes 196616 | tf_op jit(solution)/shard_map/ppermute | solution.py:217
  62.3 11.2 %collective-permute-start.14 = (f32[192,128]{1,0:T(8,128)S(1)}, f32[192,128]{1,0:T(8,128)S(1)}, u32[]{:S(2)}, u32[]{:S(2)}) collective-permute-start(f32[192,128]{1,0:T(8,128)S(1)} %get-tuple-element.63), channel_id=1, source_target_pairs={{0,2},{1,3},{2,4},{3,5},{4,6},{5,7},{6,8},{7,9},{8,10},{9,11},{10,... | collective-permute-start | bytes 294920 | tf_op jit(solution)/shard_map/ppermute | solution.py:214
  62.3 19.7 %collective-permute-start.10 = (f32[256,128]{1,0:T(8,128)S(1)}, f32[256,128]{1,0:T(8,128)S(1)}, u32[]{:S(2)}, u32[]{:S(2)}) collective-permute-start(f32[256,128]{1,0:T(8,128)S(1)} %get-tuple-element.58), channel_id=1, source_target_pairs={{0,1},{1,2},{2,3},{3,4},{4,5},{5,6},{6,7},{7,8},{8,9},{9,10},{10,1... | collective-permute-start | bytes 393224 | tf_op jit(solution)/shard_map/ppermute | solution.py:214
  62.4 19.6 %collective-permute-start.11 = (f32[256,128]{1,0:T(8,128)S(1)}, f32[256,128]{1,0:T(8,128)S(1)}, u32[]{:S(2)}, u32[]{:S(2)}) collective-permute-start(f32[256,128]{1,0:T(8,128)S(1)} %get-tuple-element.59), channel_id=1, source_target_pairs={{0,31},{1,0},{2,1},{3,2},{4,3},{5,4},{6,5},{7,6},{8,7},{9,8},{10,9... | collective-permute-start | bytes 393224 | tf_op jit(solution)/shard_map/ppermute | solution.py:217
  68.1 16.8 %collective-permute-start.4 = (f32[128,256]{1,0:T(8,128)S(1)}, f32[128,256]{1,0:T(8,128)S(1)}, u32[]{:S(2)}, u32[]{:S(2)}) collective-permute-start(f32[128,256]{1,0:T(8,128)S(1)} %get-tuple-element.49), channel_id=1, source_target_pairs={{0,1},{1,2},{2,3},{3,4},{4,5},{5,6},{6,7},{7,8},{8,9},{9,10},{10,1... | collective-permute-start | bytes 393224 | tf_op jit(solution)/shard_map/ppermute | solution.py:214
  68.1 16.8 %collective-permute-start.5 = (f32[128,256]{1,0:T(8,128)S(1)}, f32[128,256]{1,0:T(8,128)S(1)}, u32[]{:S(2)}, u32[]{:S(2)}) collective-permute-start(f32[128,256]{1,0:T(8,128)S(1)} %get-tuple-element.50), channel_id=1, source_target_pairs={{0,31},{1,0},{2,1},{3,2},{4,3},{5,4},{6,5},{7,6},{8,7},{9,8},{10,9... | collective-permute-start | bytes 393224 | tf_op jit(solution)/shard_map/ppermute | solution.py:217
  73.5 4.6 %collective-permute-start.15 = (f32[192,128]{1,0:T(8,128)S(1)}, f32[192,128]{1,0:T(8,128)S(1)}, u32[]{:S(2)}, u32[]{:S(2)}) collective-permute-start(f32[192,128]{1,0:T(8,128)S(1)} %get-tuple-element.64), channel_id=1, source_target_pairs={{0,30},{1,31},{2,0},{3,1},{4,2},{5,3},{6,4},{7,5},{8,6},{9,7},{10,... | collective-permute-start | bytes 294920 | tf_op jit(solution)/shard_map/ppermute | solution.py:217
where the time goes:
time: 94.4 us; the launch traced here: 94.1 us
  starting transfers between devices  39.2 us (42%)
  Pallas kernels  27.9 us (30%)
  waiting for transfers between devices  19.3 us (20%)
  local copies, waits for them, and re-layouts  6.82 us (7%)
    ppermute x8, starting transfers between devices, left(): lax.ppermute(v, AXES, [(i, (i - d) % devices) for i in range(devices)])  38.9 us
    pallas_call x8, Pallas kernels, kernel_call(): pl.pallas_call(fn, out_shape=[jax.ShapeDtypeStruct(o, F32) for o in outs]...  27.9 us
    ppermute x8, waiting for transfers between devices, right(): lax.ppermute(v, AXES, [(i, (i + d) % devices) for i in range(devices)])  11.9 us
    ppermute x8, waiting for transfers between devices, left(): lax.ppermute(v, AXES, [(i, (i - d) % devices) for i in range(devices)])  7.41 us
    unnamed x14, local copies, waits for them, and re-layouts  4.13 us
    slice x2, local copies, waits for them, and re-layouts, edges_of(): return jnp.concatenate([pressure[:, i, :], stiffness[:, i, :]], axis=0)  2.68 us
  transfers between devices with their start and end apart: 16, of which 7 were waited for; matrix products, arithmetic and copies ran while one was open for 0% of the time, Pallas kernels for 16%

commit v1 on v0

--- a/solution.py
+++ b/solution.py
@@ -162,7 +162,7 @@
 
 
 VM = pl.BlockSpec(memory_space=pltpu.VMEM)
-ANY = pl.BlockSpec(memory_space=pl.ANY)
+ANY = pl.BlockSpec(memory_space=pltpu.HBM)
 
 
 def lane_halves(ref, buf, sems, inward):
@@ -210,22 +210,31 @@
     ext = [(span[lev], lanes[lev]) for lev in range(4)]
     own = [(pos[lev] * z, lanes[lev]) for lev in range(4)]
 
-    def right(v, d=1):
-        return lax.ppermute(v, AXES, [(i, (i + d) % devices) for i in range(devices)])
-
-    def left(v, d=1):
-        return lax.ppermute(v, AXES, [(i, (i - d) % devices) for i in range(devices)])
+    def swap(v, d, odd):
+        pairs = []
+        for i in range(devices):
+            up = (i // d + odd) % 2 == 0
+            pairs.append((i, (i + (d if up else -d)) % devices))
+        return lax.ppermute(v, AXES, pairs)
+
+    def exchange(odd_side, even_side, d=1):
+        return swap(odd_side, d, 1), swap(even_side, d, 0)
+
+    def low_first(d=1):
+        return 1 - lax.rem(lax.axis_index(AXES[1]) // d, 2)
+
+    def inner(n, first):
+        edge = (1 - first) * (n - 1)
+        return ((edge, 2 * first - 1), ((n - 1) - edge, 1 - 2 * first))
+
+    def outer(n, first):
+        edge = n - first * (n + 1)
+        return ((edge, 1 - 2 * first), ((n - 1) - edge, 2 * first - 1))
 
     flat = [v.reshape(z * n0, r0) for v in (pressure, forcing, stiffness)]
 
-    def edges_of(i):
-        return jnp.concatenate([pressure[:, i, :], stiffness[:, i, :]], axis=0)
-
-    first, last = edges_of(0), edges_of(n0 - 1)
-    pk_from_right, pk_from_left = left(first), right(last)
-
     def start_kernel(
-        p, f, k, v, c, ke, se, re, de, to_left, to_right, pb, kbuf, pbuf, fbuf, ksem, psem, fsem
+        p, f, k, v, c, ke, se, re, de, to_o, to_e, pb, kbuf, pbuf, fbuf, ksem, psem, fsem
     ):
         copies = [
             lane_halves(far, buf, sem, True)
@@ -240,7 +249,6 @@
         v3 = column_matrix(v[...])
         pb.put(-1, jnp.zeros((z, r0), F32))
         pb.put(n0, jnp.zeros((z, r0), F32))
-
         for pair in copies[:2]:
             for copy in pair:
                 copy.wait()
@@ -253,7 +261,6 @@
                 pb.put(i + j, block_rows(pbuf, i + j, z, n0))
 
         over(0, n0, 4, load)
-
         for copy in copies[2]:
             copy.wait()
 
@@ -269,99 +276,137 @@
                 de.put(q, column_apply(m3, se.get(q) * rv))
 
         over(0, n0, 4, start)
-        for out, q, step in ((to_left, 0, 1), (to_right, n0 - 1, -1)):
-            out[:z, :] = re.get(q)
-            out[z:, :] = de.get(q + step)
-
-    k_ext, s_ext, r_ext, d_ext, rd_left, rd_right = kernel_call(
+        for out, (q, step) in zip((to_o, to_e), inner(n0, low_first())):
+            out = Field(out, z, 0)
+            for i, v in enumerate((pb.get(q), ke.get(q), re.get(q), de.get(q + step))):
+                out.put(i, v)
+
+    k_ext, s_ext, r_ext, d_ext, e_o, e_e = kernel_call(
         start_kernel,
-        [ext[0]] * 4 + [(2 * z, r0)] * 2,
+        [ext[0]] * 4 + [(4 * z, r0)] * 2,
         [((n0 + 2) * z, r0)] + [(2, z * n0, LANES)] * 3,
         [*flat, vertical_op, col_inverse],
         far_in=3,
         sems=(2, 2, 2),
     )
-    rd_from_right, rd_from_left = left(rd_left), right(rd_right)
-
-    def stiff_kernel(ke, k1, k2, k3, to_left, to_right):
+    with jax.named_scope("edge"):
+        from_o, from_e = exchange(e_o, e_e)
+
+    def stiff_kernel(ke, k1, k2, k3, to_o, to_e):
         ke = Field(ke, z, halo[0])
         ks = [ke] + [Field(x, z, 0) for x in (k1, k2, k3)]
         for lev in range(3):
             matrix = lane_matrix(lanes[lev], lanes[lev + 1], 1.0 / 16.0, False)
             coarsen(ks[lev], ks[lev + 1], matrix, 0, pos[lev + 1])
-        for out, at in ((to_left, lambda i, n: i), (to_right, lambda i, n: n - 1 - i)):
+        first = low_first()
+        for out, (q, step), (q1, step1) in zip((to_o, to_e), inner(n0, first), inner(n1, first)):
             out = Field(out, z, 0)
-            k01 = ke.get(at(1, n0))
+            k01 = ke.get(q + step)
             out.put(0, k01[:, :LANES])
             out.put(1, k01[:, LANES:])
             for i in range(3):
-                out.put(2 + i, ks[1].get(at(i, n1)))
+                out.put(2 + i, ks[1].get(q1 + i * step1))
             for i in range(2):
                 out.put(5 + i, packed([ks[2].get(2 * i + j) for j in range(2)], valid[2]))
 
-    k1, k2, k3, ks_left, ks_right = kernel_call(
+    k1, k2, k3, ks_o, ks_e = kernel_call(
         stiff_kernel, own[1:] + [(7 * z, LANES)] * 2, [], [k_ext]
     )
-    ks_from_right, ks_from_left = left(ks_left), right(ks_right)
+    with jax.named_scope("stiff"):
+        ks_from_o, ks_from_e = exchange(ks_o, ks_e)
+
+    def inner_kernel(k1, c, ke, se, de, re_i, re, d2, c0, b1, d1):
+        ke, se, re, de, d2 = (Field(x, z, halo[0]) for x in (ke, se, re, de, d2))
+        re_i = Field(re_i, z, halo[0])
+        c0, k1 = (Field(x, z, 0) for x in (c0, k1))
+        b1, d1 = (Field(x, z, halo[1]) for x in (b1, d1))
+        m3 = column_matrix(c[0])
+        m1 = column_matrix(c[1])
+        sweep(re, de, d2, ke, se, m3, 0, valid[0], 2, n0 - 2, 4)
+        residue(re, d2, ke, se, 0, valid[0], 3, n0 - 3, 2)
+        over(2, n0 - 2, 4, lambda i, n: c0.put(i, de.get(i, n) + d2.get(i, n), n))
+        coarsen(re, b1, lane_matrix(lanes[0], lanes[1], 0.25, False), 2, n1 - 2)
+        for i in range(2, n1 - 2):
+            d1.put(i, column_apply(m1, scaling(k1.get(i), 1) * b1.get(i)))
+
+    r_ext, d2_ext, c0, b1, d1 = kernel_call(
+        inner_kernel,
+        [ext[0]] * 2 + [own[0], ext[1], ext[1]],
+        [],
+        [k1, col_inverse, k_ext, s_ext, d_ext, r_ext],
+        {5: 0},
+    )
 
     def fine_kernel(
-        first, last, pk_l, pk_r, rd_l, rd_r, k1, c, ke_i, se_i, re_i, de_i,
-        ke, se, re, de, c0, b1, d1, to_left, to_right, r_left, r_right, d2
+        e_o, e_e, m_o, m_e, k1, c, ke_i, se_i, re_i, de, d2_i, c0_i, b1_i, d1_i,
+        ke, se, re, d2, c0, b1, d1, to_o, to_e, r_o, r_e
     ):
         ke, se, re, de, d2 = (Field(x, z, halo[0]) for x in (ke, se, re, de, d2))
+        c0, k1 = (Field(x, z, 0) for x in (c0, k1))
+        b1, d1 = (Field(x, z, halo[1]) for x in (b1, d1))
         m3 = column_matrix(c[0])
-        for mine, pk, rd, q, step in (
-            (first, pk_l, rd_l, 0, -1),
-            (last, pk_r, rd_r, n0 - 1, 1),
-        ):
-            h = q + step
-            kh = pk[z:, :]
+        m1 = column_matrix(c[1])
+        first = low_first()
+        d2.put(-2, jnp.zeros((z, r0), F32))
+        for mine, got, (h, step) in zip((e_o, e_e), (m_o, m_e), outer(n0, first)):
+            mine, got = Field(mine, z, 0), Field(got, z, 0)
+            q = h - step
+            kh = got.get(1)
             ke.put(h, kh)
             se.put(h, scaling(kh, 0))
-            re.put(h, rd[:z, :] + kh * mine[:z, :])
-            re.put(q, re.get(q) + ke.get(q) * pk[:z, :])
+            re.put(h, got.get(2) + kh * mine.get(0))
+            re.put(q, mine.get(2) + mine.get(1) * got.get(0))
+            de.put(h + step, got.get(3))
+        for h, q in ((-1, 0), (n0, n0 - 1)):
             for at in (h, q):
                 de.put(at, column_apply(m3, se.get(at) * re.get(at)))
-            de.put(h + step, rd[z:, :])
-        sweep(re, de, d2, ke, se, m3, 0, valid[0], -1, n0 + 1, 3)
-        residue(re, d2, ke, se, 0, valid[0], 0, n0, 2)
-        c0 = Field(c0, z, 0)
-        over(0, n0, 4, lambda i, n: c0.put(i, de.get(i, n) + d2.get(i, n), n))
-        b1 = Field(b1, z, halo[1])
-        coarsen(re, b1, lane_matrix(lanes[0], lanes[1], 0.25, False), 0, n1)
-        d1 = Field(d1, z, halo[1])
-        k1 = Field(k1, z, 0)
-        m1 = column_matrix(c[1])
-        for i in range(n1):
-            d1.put(i, column_apply(m1, scaling(k1.get(i), 1) * b1.get(i)))
-        for out, q, step in ((to_left, 0, 1), (to_right, n1 - 1, -1)):
+        for q in (-1, n0 - 2):
+            sweep(re, de, d2, ke, se, m3, 0, valid[0], q, q + 3, 3)
+        for q in (0, n0 - 3):
+            residue(re, d2, ke, se, 0, valid[0], q, q + 3, 3)
+        for q in (0, n0 - 2):
+            c0.put(q, de.get(q, 2) + d2.get(q, 2), 2)
+        matrix = lane_matrix(lanes[0], lanes[1], 0.25, False)
+        for q in (0, n1 - 2):
+            coarsen(re, b1, matrix, q, q + 2)
+            for i in (q, q + 1):
+                d1.put(i, column_apply(m1, scaling(k1.get(i), 1) * b1.get(i)))
+        for out, (q, step) in zip((to_o, to_e), inner(n1, first)):
             out[:z, :] = b1.get(q)
             out[z:, :] = d1.get(q + step)
-        for out, q, step in ((r_left, 0, 1), (r_right, n0 - 1, -1)):
+        for out, (q, step) in zip((r_o, r_e), inner(n0, first)):
             out[:z, :] = re.get(q)
             out[z:, :] = re.get(q + step)
 
-    k_ext, s_ext, r_ext, d_ext, c0, b1, d1, bd_left, bd_right, r_left, r_right = kernel_call(
-        fine_kernel,
-        [ext[0]] * 4 + [own[0], ext[1], ext[1]] + [(2 * z, lanes[1])] * 2 + [(2 * z, r0)] * 2,
-        [ext[0]],
-        [first, last, pk_from_left, pk_from_right, rd_from_left, rd_from_right, k1, col_inverse,
-         k_ext, s_ext, r_ext, d_ext],
-        {8: 0, 9: 1, 10: 2, 11: 3},
-    )
-    bd_from_right, bd_from_left = left(bd_left), right(bd_right)
-    r_from_right, r_from_left = left(r_left), right(r_right)
+    def fine_edges(e_o, e_e, m_o, m_e, k1, c, ke_i, se_i, re_i, de_i, d2_i, c0_i, b1_i, d1_i,
+                   ke, se, re, de, d2, c0, b1, d1, to_o, to_e, r_o, r_e):
+        fine_kernel(e_o, e_e, m_o, m_e, k1, c, ke_i, se_i, re_i, de, d2_i, c0_i, b1_i, d1_i,
+                    ke, se, re, d2, c0, b1, d1, to_o, to_e, r_o, r_e)
+
+    k_ext, s_ext, r_ext, _, _, c0, b1, d1, bd_o, bd_e, r_o, r_e = kernel_call(
+        fine_edges,
+        [ext[0]] * 5 + [own[0], ext[1], ext[1]] + [(2 * z, lanes[1])] * 2 + [(2 * z, r0)] * 2,
+        [],
+        [e_o, e_e, from_o, from_e, k1, col_inverse,
+         k_ext, s_ext, r_ext, d_ext, d2_ext, c0, b1, d1],
+        {6: 0, 7: 1, 8: 2, 9: 3, 10: 4, 11: 5, 12: 6, 13: 7},
+    )
+    with jax.named_scope("second"):
+        bd_from_o, bd_from_e = exchange(bd_o, bd_e)
+    with jax.named_scope("res0"):
+        r_from_o, r_from_e = exchange(r_o, r_e)
 
     def second_kernel(
-        bd_l, bd_r, ks_l, ks_r, k1_i, k2_i, c, b1_i, d1_i,
-        b1, d1, k1, s1, b2, to_left, to_right, m_left, m_right, d2
+        bd_o, bd_e, ks_o, ks_e, k1_i, k2_i, c, b1_i, d1_i,
+        b1, d1, k1, s1, b2, to, m_o, m_e, d2
     ):
         b1, d1, k1, s1, d2 = (Field(x, z, halo[1]) for x in (b1, d1, k1, s1, d2))
         b2 = Field(b2, z, halo[2])
         k1_i = Field(k1_i, z, 0)
         m3 = column_matrix(c[1])
+        first = low_first()
         k1.put(0, k1_i.get(0, n1), n1)
-        for ks, bd, q, step in ((ks_l, bd_l, -1, -1), (ks_r, bd_r, n1, 1)):
+        for ks, bd, (q, step) in zip((ks_o, ks_e), (bd_o, bd_e), outer(n1, first)):
             ks = Field(ks, z, 0)
             for i in range(3):
                 k1.put(q + i * step, ks.get(2 + i))
@@ -375,33 +420,35 @@
         coarsen(b1, b2, lane_matrix(lanes[1], lanes[2], 0.25, False), 0, n2)
         for i in range(2):
             both = packed([b2.get(2 * i + j) for j in range(2)], valid[2])
-            for out in (to_left, to_right):
-                out[i * z : (i + 1) * z, :] = both
-        for out, q, step in ((m_left, 0, 1), (m_right, n1 - 1, -1)):
+            to[i * z : (i + 1) * z, :] = both
+        for out, (q, step) in zip((m_o, m_e), inner(n1, first)):
             out = Field(out, z, 0)
             for i in range(3):
                 out.put(i, b1.get(q + i * step))
             out.put(3, d2.get(q + step))
         d1.put(-1, d1.get(-1, n1 + 2) + d2.get(-1, n1 + 2), n1 + 2)
 
-    r1, c1, k1e, s1e, b2, b2_left, b2_right, m_left, m_right = kernel_call(
+    r1, c1, k1e, s1e, b2, b2_own, m_o, m_e = kernel_call(
         second_kernel,
-        [ext[1]] * 4 + [ext[2]] + [(n2 // 2 * z, LANES)] * 2 + [(4 * z, LANES)] * 2,
+        [ext[1]] * 4 + [ext[2]] + [(n2 // 2 * z, LANES)] + [(4 * z, LANES)] * 2,
         [ext[1]],
-        [bd_from_left, bd_from_right, ks_from_left, ks_from_right, k1, k2, col_inverse, b1, d1],
+        [bd_from_o, bd_from_e, ks_from_o, ks_from_e, k1, k2, col_inverse, b1, d1],
         {7: 0, 8: 1},
     )
-    b2_from_right, b2_from_left = left(b2_left), right(b2_right)
-    m_from_right, m_from_left = left(m_left), right(m_right)
+    with jax.named_scope("third"):
+        b2_from_o, b2_from_e = exchange(b2_own, b2_own)
+    with jax.named_scope("res1"):
+        m_from_o, m_from_e = exchange(m_o, m_e)
 
     def third_kernel(
-        b2_l, b2_r, ks_l, ks_r, k2_i, c, b2_i, b2, d1, k2, s2, w3, to_left, to_right, d2
+        b2_o, b2_e, ks_o, ks_e, k2_i, c, b2_i, b2, d1, k2, s2, w3, to_o, to_e, d2
     ):
         b2, d1, k2, s2, d2 = (Field(x, z, halo[2]) for x in (b2, d1, k2, s2, d2))
         k2_i = Field(k2_i, z, 0)
         m3 = column_matrix(c[2])
         k2.put(0, k2_i.get(0, n2), n2)
-        for ks, b, base in ((ks_l, b2_l, -n2), (ks_r, b2_r, n2)):
+        first = low_first()
+        for ks, b, base in ((ks_o, b2_o, n2 - 2 * n2 * first), (ks_e, b2_e, 2 * n2 * first - n2)):
             ks, b = Field(ks, z, 0), Field(b, z, 0)
             for i in range(n2):
                 b2.put(base + i, unpacked(b.get(i // 2), i % 2, valid[2]))
@@ -419,30 +466,32 @@
                 for i in range(-1, n3 + 1)
             ]
             w3.put(to, packed(rows, valid[3]))
-        for out, q in ((to_left, -2), (to_right, n2 + 1)):
+        for out, (q, step) in zip((to_o, to_e), outer(n2, low_first(2))):
             out = Field(out, z, 0)
             out.put(0, w3.get(0))
             out.put(1, w3.get(1))
-            out.put(2, b2.get(q))
+            out.put(2, b2.get(q + step))
         d1.put(-2, d1.get(-2, n2 + 4) + d2.get(-2, n2 + 4), n2 + 4)
 
-    r2, c2, k2e, s2e, w3, w_left, w_right = kernel_call(
+    r2, c2, k2e, s2e, w3, w_o, w_e = kernel_call(
         third_kernel,
         [ext[2]] * 4 + [(2 * z, LANES)] + [(3 * z, LANES)] * 2,
         [ext[2]],
-        [b2_from_left, b2_from_right, ks_from_left, ks_from_right, k2, col_inverse, b2],
+        [b2_from_o, b2_from_e, ks_from_o, ks_from_e, k2, col_inverse, b2],
         {6: 0},
     )
-    w_from_right, w_from_left = left(w_left, 2), right(w_right, 2)
-
-    def coarse_kernel(w_l, w_r, w, c, v, c2, k2, s2, r2_i, r2, e2, b3, k3, s3, da, db, e3, d3, g3, d4, d5):
+    with jax.named_scope("coarse"):
+        w_from_o, w_from_e = exchange(w_o, w_e, 2)
+
+    def coarse_kernel(w_o, w_e, w, c, v, c2, k2, s2, r2_i, r2, e2, b3, k3, s3, da, db, e3, d3, g3, d4, d5):
         b3, k3, s3, da, db, e3 = (Field(x, z, halo[3]) for x in (b3, k3, s3, da, db, e3))
         c2, k2, s2, r2, e2, d3, g3, d4, d5 = (
             Field(x, z, halo[2]) for x in (c2, k2, s2, r2, e2, d3, g3, d4, d5)
         )
         m3 = column_matrix(c[3])
         v3 = column_matrix(v[...])
-        for src, base in ((w_l, -5), (w, -1), (w_r, 3)):
+        first = low_first(2)
+        for src, base in ((w_o, 3 - 8 * first), (w, -1), (w_e, 8 * first - 5)):
             src = Field(src, z, 0)
             bv, kv = src.get(0), src.get(1)
             for i in range(4):
@@ -456,8 +505,8 @@
             sweep(b3, da, db, k3, s3, m3, 3, valid[3], -reach, n3 + reach, 5)
             e3.put(-2, e3.get(-2, n3 + 4) + db.get(-2, n3 + 4), n3 + 4)
             da, db = db, da
-        r2.put(-3, Field(w_l, z, 0).get(2))
-        r2.put(n2 + 2, Field(w_r, z, 0).get(2))
+        for src, (q, step) in zip((w_o, w_e), outer(n2, first)):
+            r2.put(q + 2 * step, Field(src, z, 0).get(2))
         m2 = column_matrix(c[2])
         refine(e3, v3, lane_matrix(lanes[3], lanes[2], 1.0, True), d3, g3, -2, n3 + 2)
         after_coarse(r2, d3, g3, d4, k2, s2, m2, valid[2], -3, n2 + 3, 5)
@@ -469,39 +518,39 @@
         coarse_kernel,
         [ext[2]] * 2,
         [ext[3]] * 6 + [ext[2]] * 4,
-        [w_from_left, w_from_right, w3, col_inverse, vertical_op, c2, k2e, s2e, r2],
+        [w_from_o, w_from_e, w3, col_inverse, vertical_op, c2, k2e, s2e, r2],
         {8: 0},
     )
 
-    def second_up_kernel(m_l, m_r, c, v, e2, k1, s1, c1, r1_i, r1, e1, d3, g3, d4, d5):
+    def second_up_kernel(m_o, m_e, c, v, e2, k1, s1, c1, r1_i, r1, e1, d3, g3, d4, d5):
         e2 = Field(e2, z, halo[2])
         k1, s1, c1, r1, e1, d3, g3, d4, d5 = (
             Field(x, z, halo[1]) for x in (k1, s1, c1, r1, e1, d3, g3, d4, d5)
         )
         m1 = column_matrix(c[1])
         v3 = column_matrix(v[...])
-        for m, q, step in ((m_l, -1, -1), (m_r, n1, 1)):
-            m = Field(m, z, 0)
+        sides = tuple(zip((m_o, m_e), outer(n1, low_first())))
+        for m, (q, step) in sides:
             for i in range(3):
-                r1.put(q + i * step, m.get(i))
+                r1.put(q + i * step, Field(m, z, 0).get(i))
         refine(e2, v3, lane_matrix(lanes[2], lanes[1], 1.0, True), d3, g3, -2, n2 + 2)
         after_coarse(r1, d3, g3, d4, k1, s1, m1, valid[1], -3, n1 + 3, 7)
         sweep(r1, d4, d5, k1, s1, m1, 1, valid[1], -2, n1 + 2, 6)
         q, n = -2, n1 + 4
         e1.put(q, c1.get(q, n) + d3.get(q, n) + d4.get(q, n) + d5.get(q, n), n)
-        for m, at in ((m_l, -2), (m_r, n1 + 1)):
-            e1.put(at, e1.get(at) + Field(m, z, 0).get(3))
+        for m, (q, step) in sides:
+            e1.put(q + step, e1.get(q + step) + Field(m, z, 0).get(3))
 
     _, e1 = kernel_call(
         second_up_kernel,
         [ext[1]] * 2,
         [ext[1]] * 4,
-        [m_from_left, m_from_right, col_inverse, vertical_op, e2, k1e, s1e, c1, r1],
+        [m_from_o, m_from_e, col_inverse, vertical_op, e2, k1e, s1e, c1, r1],
         {8: 0},
     )
 
     def last_kernel(
-        p, r_l, r_r, ks_l, ks_r, c, v, e1, c0, ke_i, se_i, re_i,
+        p, r_o, r_e, ks_o, ks_e, c, v, e1, c0, ke_i, se_i, re_i,
         ke, se, re, up, res, d3, g3, d4, d5, pbuf, ubuf, vbuf, psem, usem, vsem
     ):
         loads = lane_halves(p, pbuf, psem, True)
@@ -513,7 +562,7 @@
         c0 = Field(c0, z, 0)
         m3 = column_matrix(c[0])
         v3 = column_matrix(v[...])
-        for r, ks, q, step in ((r_l, ks_l, -1, -1), (r_r, ks_r, n0, 1)):
+        for r, ks, (q, step) in zip((r_o, r_e), (ks_o, ks_e), outer(n0, low_first())):
             re.put(q, r[:z, :])
             re.put(q + step, r[z:, :])
             ks = Field(ks, z, 0)
@@ -555,7 +604,7 @@
         last_kernel,
         [ext[0]] * 3 + [(z * n0, r0)] * 2,
         [((n0 + 8) * z, r0)] * 2 + [ext[0]] * 2 + [(2, z * n0, LANES)] * 3,
-        [flat[0], r_from_left, r_from_right, ks_from_left, ks_from_right, col_inverse, vertical_op,
+        [flat[0], r_from_o, r_from_e, ks_from_o, ks_from_e, col_inverse, vertical_op,
          e1, c0, k_ext, s_ext, r_ext],
         {9: 0, 10: 1, 11: 2},
         far_in=1,

time: 94.4 us -> 82.2 us (0.87)
  starting transfers between devices: 39.2 us -> 17 us
  waiting for transfers between devices: 19.3 us -> 31.2 us
  local copies, waits for them, and re-layouts: 6.82 us -> 5.34 us
    ppermute x16 -> x14, starting transfers between devices: 39.2 us -> 17 us  [swap(): return lax.ppermute(v, AXES, pairs)]
    ppermute x16 -> x14, waiting for transfers between devices: 19.3 us -> 31.2 us  [swap(): return lax.ppermute(v, AXES, pairs)]
    slice x2 -> x0, local copies, waits for them, and re-layouts: 2.68 us -> none  [edges_of(): return jnp.concatenate([pressure[:, i, :], stiffness[:, i, :]], axis=0)]
    unnamed x14 -> x16, local copies, waits for them, and re-layouts: 4.13 us -> 5.34 us
    pallas_call x8 -> x9, Pallas kernels: 27.9 us -> 27.6 us  [kernel_call(): pl.pallas_call(fn, out_shape=[jax.ShapeDtypeStruct(o, F32) for o in outs]...]
  transfers between devices with their start and end apart: 16 -> 14, of which waited for: 7 -> 8; matrix products, arithmetic and copies ran while one was open for 0% -> 0% of each run, Pallas kernels for 16% -> 15%
where the time goes in v1:
time: 82.2 us; the launch traced here: 81.9 us
  waiting for transfers between devices  31.2 us (38%)
  Pallas kernels  27.6 us (34%)
  starting transfers between devices  17 us (21%)
  local copies, waits for them, and re-layouts  5.34 us (6%)
    ppermute x14, waiting for transfers between devices, swap(): return lax.ppermute(v, AXES, pairs)  31.2 us
    pallas_call x9, Pallas kernels, kernel_call(): pl.pallas_call(fn, out_shape=[jax.ShapeDtypeStruct(o, F32) for o in outs]...  27.6 us
    ppermute x14, starting transfers between devices, swap(): return lax.ppermute(v, AXES, pairs)  17 us
    unnamed x16, local copies, waits for them, and re-layouts  5.34 us
  transfers between devices with their start and end apart: 14, of which 8 were waited for; matrix products, arithmetic and copies ran while one was open for 0% of the time, Pallas kernels for 15%

profile of v1, /device:TPU:0, one launch (start us, length us, event | category | flops | bytes accessed | tf_op | source)
XLA Modules:
  0.0 81.9 jit_solution(15788878260128758573)
XLA Ops:
  0.6 0.0 copy-start
  0.6 0.9 %copy-done = f32[4,64,64]{2,1,0:T(8,128)S(1)} copy-done((f32[4,64,64]{2,1,0:T(8,128)S(1)}, f32[4,64,64]{2,1,0:T(8,128)}, u32[]{:S(2)}) %copy-start) | copy-done | bytes 65560
  1.5 0.0 copy-start.2
  1.5 1.2 %copy-done.2 = f32[64,16,256]{2,1,0:T(8,128)S(1)} copy-done((f32[64,16,256]{2,1,0:T(8,128)S(1)}, f32[64,16,256]{2,1,0:T(8,128)}, u32[]{:S(2)}) %copy-start.2) | copy-done | bytes 1048600
  2.8 0.0 copy-start.4
  2.8 1.2 %copy-done.4 = f32[64,16,256]{2,1,0:T(8,128)S(1)} copy-done((f32[64,16,256]{2,1,0:T(8,128)S(1)}, f32[64,16,256]{2,1,0:T(8,128)}, u32[]{:S(2)}) %copy-start.4) | copy-done | bytes 1048600
  4.0 0.0 copy-start.5
  4.0 1.2 %copy-done.5 = f32[64,16,256]{2,1,0:T(8,128)S(1)} copy-done((f32[64,16,256]{2,1,0:T(8,128)S(1)}, f32[64,16,256]{2,1,0:T(8,128)}, u32[]{:S(2)}) %copy-start.5) | copy-done | bytes 1048600
  5.2 0.0 copy-start.6
  5.2 0.8 copy-done.6
  6.0 3.4 %start_kernel.1 = (f32[1280,256]{1,0:T(8,128)S(1)}, f32[1280,256]{1,0:T(8,128)S(1)}, f32[1280,256]{1,0:T(8,128)S(1)}, f32[1280,256]{1,0:T(8,128)S(1)}, f32[256,256]{1,0:T(8,128)S(1)}, /*index=5*/f32[256,256]{1,0:T(8,128)S(1)}) custom-call(f32[1024,256]{1,0:T(8,128)S(1)} %bitcast.5, f32[1024,256]{1,0:T(8,128)S(1)} %bitcast.7, f32[1024,256]{1,0:T(8,128)S(1)} %bitcast.8, ...), custom_call_target="tpu_custom_call" | custom-call | tf_op jit(solution)/shard_map/start_kernel/pallas_call | solution.py:189
  9.3 6.5 %collective-permute-start = (f32[256,256]{1,0:T(8,128)S(1)}, f32[256,256]{1,0:T(8,128)S(1)}, u32[]{:S(2)}, u32[]{:S(2)}) collective-permute-start(f32[256,256]{1,0:T(8,128)S(1)} %get-tuple-element.46.e_o), channel_id=1, source_target_pairs={{0,31},{1,2},{2,1},{3,4},{4,3},{5,6},{6,5},{7,8},{8,7},{9,10},{10,... | collective-permute-start | bytes 786440 | tf_op jit(solution)/shard_map/edge/ppermute | solution.py:218
  15.8 0.0 collective-permute-start.1
  15.8 1.2 %stiff_kernel.1 = (f32[512,128]{1,0:T(8,128)S(1)}, f32[256,128]{1,0:T(8,128)S(1)}, f32[128,128]{1,0:T(8,128)}, f32[448,128]{1,0:T(8,128)S(1)}, f32[448,128]{1,0:T(8,128)S(1)}) custom-call(f32[1280,256]{1,0:T(8,128)S(1)} %get-tuple-element.48.ke.ke_i), custom_call_target="tpu_custom_call" | custom-call | tf_op jit(solution)/shard_map/stiff_kernel/pallas_call | solution.py:189
  17.0 1.4 %collective-permute-start.4 = (f32[448,128]{1,0:T(8,128)S(1)}, f32[448,128]{1,0:T(8,128)S(1)}, u32[]{:S(2)}, u32[]{:S(2)}) collective-permute-start(f32[448,128]{1,0:T(8,128)S(1)} %get-tuple-element.60), channel_id=1, source_target_pairs={{0,31},{1,2},{2,1},{3,4},{4,3},{5,6},{6,5},{7,8},{8,7},{9,10},{10,... | collective-permute-start | bytes 688136 | tf_op jit(solution)/shard_map/stiff/ppermute | solution.py:218
  18.3 0.7 collective-permute-start.5
  19.0 0.0 copy-start.1
  19.0 2.6 %inner_kernel.1 = (f32[1280,256]{1,0:T(8,128)S(1)}, f32[1280,256]{1,0:T(8,128)S(1)}, f32[1024,256]{1,0:T(8,128)S(1)}, f32[1024,128]{1,0:T(8,128)S(1)}, f32[1024,128]{1,0:T(8,128)S(1)}) custom-call(f32[512,128]{1,0:T(8,128)S(1)} %get-tuple-element.49.k1.k1_i, f32[4,64,64]{2,1,0:T(8,128)S(1)} %copy-done, ...), custom_call_target="tpu_custom_call", output_to_operand_aliasing={{0}: (5, {})} | custom-call | tf_op jit(solution)/shard_map/inner_kernel/pallas_call | solution.py:189
  21.6 1.0 %collective-permute-done.m_o = f32[256,256]{1,0:T(8,128)S(1)} collective-permute-done((f32[256,256]{1,0:T(8,128)S(1)}, f32[256,256]{1,0:T(8,128)S(1)}, u32[]{:S(2)}, u32[]{:S(2)}) %collective-permute-start) | collective-permute-done | bytes 262176 | tf_op jit(solution)/shard_map/edge/ppermute | solution.py:218
  22.6 10.7 %collective-permute-done.1.m_e = f32[256,256]{1,0:T(8,128)S(1)} collective-permute-done((f32[256,256]{1,0:T(8,128)S(1)}, f32[256,256]{1,0:T(8,128)S(1)}, u32[]{:S(2)}, u32[]{:S(2)}) %collective-permute-start.1) | collective-permute-done | bytes 262176 | tf_op jit(solution)/shard_map/edge/ppermute | solution.py:218
  33.2 0.0 copy-done.1
  33.2 1.2 %fine_edges.1 = (f32[1280,256]{1,0:T(8,128)S(1)}, f32[1280,256]{1,0:T(8,128)S(1)}, f32[1280,256]{1,0:T(8,128)S(1)}, f32[1280,256]{1,0:T(8,128)S(1)}, f32[1280,25...) custom-call(f32[256,256]{1,0:T(8,128)S(1)} %get-tuple-element.46.e_o, ...), custom_call_target="tpu_custom_call", output_to_operand_aliasing={{0}: (6, {}), {1}: (7, {}), {2}: (8, {}), {3}: (9, {}), {4}... | custom-call | tf_op jit(solution)/shard_map/fine_edges/pallas_call | solution.py:189
  34.5 0.5 collective-permute-start.6
  34.9 0.0 collective-permute-start.7
  34.9 0.0 collective-permute-done.4.ks_o
  34.9 3.1 %collective-permute-done.5.ks_e = f32[448,128]{1,0:T(8,128)S(1)} collective-permute-done((f32[448,128]{1,0:T(8,128)S(1)}, f32[448,128]{1,0:T(8,128)S(1)}, u32[]{:S(2)}, u32[]{:S(2)}) %collective-permute-start.5) | collective-permute-done | bytes 229408 | tf_op jit(solution)/shard_map/stiff/ppermute | solution.py:218
  38.0 4.0 %collective-permute-done.6.bd_o = f32[128,128]{1,0:T(8,128)S(1)} collective-permute-done((f32[128,128]{1,0:T(8,128)S(1)}, f32[128,128]{1,0:T(8,128)S(1)}, u32[]{:S(2)}, u32[]{:S(2)}) %collective-permute-start.6) | collective-permute-done | bytes 65568 | tf_op jit(solution)/shard_map/second/ppermute | solution.py:218
  42.1 0.0 collective-permute-done.7.bd_e
  42.1 0.0 copy-start.7
  42.1 1.5 %second_kernel.1 = (f32[1024,128]{1,0:T(8,128)S(1)}, f32[1024,128]{1,0:T(8,128)S(1)}, f32[1024,128]{1,0:T(8,128)S(1)}, f32[1024,128]{1,0:T(8,128)S(1)}, f32[768,...) custom-call(f32[128,128]{1,0:T(8,128)S(1)} %collective-permute-done., ...), custom_call_target="tpu_custom_call", output_to_operand_aliasing={{0}: (7, {}), {1}: (8, {})} | custom-call | tf_op jit(solution)/shard_map/second_kernel/pallas_call | solution.py:189
  43.6 0.1 collective-permute-start.11
  43.7 2.3 %collective-permute-start.10 = (f32[128,128]{1,0:T(8,128)S(1)}, f32[128,128]{1,0:T(8,128)S(1)}, u32[]{:S(2)}, u32[]{:S(2)}) collective-permute-start(f32[128,128]{1,0:T(8,128)S(1)} %get-tuple-element.69), channel_id=1, source_target_pairs={{0,31},{1,2},{2,1},{3,4},{4,3},{5,6},{6,5},{7,8},{8,7},{9,10},{10,... | collective-permute-start | bytes 196616 | tf_op jit(solution)/shard_map/third/ppermute | solution.py:218
  46.0 2.0 %collective-permute-done.11.b2_e = f32[128,128]{1,0:T(8,128)S(1)} collective-permute-done((f32[128,128]{1,0:T(8,128)S(1)}, f32[128,128]{1,0:T(8,128)S(1)}, u32[]{:S(2)}, u32[]{:S(2)}) %collective-permute-start.11) | collective-permute-done | bytes 65568 | tf_op jit(solution)/shard_map/third/ppermute | solution.py:218
  47.9 3.7 %collective-permute-done.10.b2_o = f32[128,128]{1,0:T(8,128)S(1)} collective-permute-done((f32[128,128]{1,0:T(8,128)S(1)}, f32[128,128]{1,0:T(8,128)S(1)}, u32[]{:S(2)}, u32[]{:S(2)}) %collective-permute-start.10) | collective-permute-done | bytes 65568 | tf_op jit(solution)/shard_map/third/ppermute | solution.py:218
  51.6 1.7 %third_kernel.1 = (f32[768,128]{1,0:T(8,128)S(1)}, f32[768,128]{1,0:T(8,128)S(1)}, f32[768,128]{1,0:T(8,128)S(1)}, f32[768,128]{1,0:T(8,128)S(1)}, f32[128,128]{...) custom-call(f32[128,128]{1,0:T(8,128)S(1)} %collective-permute-done.10.b2_o, ...), custom_call_target="tpu_custom_call", output_to_operand_aliasing={{0}: (6, {})} | custom-call | tf_op jit(solution)/shard_map/third_kernel/pallas_call | solution.py:189
  53.3 0.1 collective-permute-start.12
  53.4 3.1 %collective-permute-start.8 = (f32[256,128]{1,0:T(8,128)S(1)}, f32[256,128]{1,0:T(8,128)S(1)}, u32[]{:S(2)}, u32[]{:S(2)}) collective-permute-start(f32[256,128]{1,0:T(8,128)S(1)} %get-tuple-element.67), channel_id=1, source_target_pairs={{0,31},{1,2},{2,1},{3,4},{4,3},{5,6},{6,5},{7,8},{8,7},{9,10},{10,... | collective-permute-start | bytes 393224 | tf_op jit(solution)/shard_map/res1/ppermute | solution.py:218
  56.5 0.0 collective-permute-start.9
  56.5 2.5 %collective-permute-start.2 = (f32[128,256]{1,0:T(8,128)S(1)}, f32[128,256]{1,0:T(8,128)S(1)}, u32[]{:S(2)}, u32[]{:S(2)}) collective-permute-start(f32[128,256]{1,0:T(8,128)S(1)} %get-tuple-element.58), channel_id=1, source_target_pairs={{0,31},{1,2},{2,1},{3,4},{4,3},{5,6},{6,5},{7,8},{8,7},{9,10},{10,... | collective-permute-start | bytes 393224 | tf_op jit(solution)/shard_map/res0/ppermute | solution.py:218
  59.0 0.0 collective-permute-start.3
  59.0 2.2 %collective-permute-done.12.w_o = f32[192,128]{1,0:T(8,128)S(1)} collective-permute-done((f32[192,128]{1,0:T(8,128)S(1)}, f32[192,128]{1,0:T(8,128)S(1)}, u32[]{:S(2)}, u32[]{:S(2)}) %collective-permute-start.12) | collective-permute-done | bytes 98336 | tf_op jit(solution)/shard_map/coarse/ppermute | solution.py:218
  61.2 0.0 collective-permute-start.13
  61.2 4.6 %collective-permute-done.13.w_e = f32[192,128]{1,0:T(8,128)S(1)} collective-permute-done((f32[192,128]{1,0:T(8,128)S(1)}, f32[192,128]{1,0:T(8,128)S(1)}, u32[]{:S(2)}, u32[]{:S(2)}) %collective-permute-start.13) | collective-permute-done | bytes 98336 | tf_op jit(solution)/shard_map/coarse/ppermute | solution.py:218
  65.8 0.0 copy-done.7
  65.8 4.0 %coarse_kernel.1 = (f32[768,128]{1,0:T(8,128)S(1)}, f32[768,128]{1,0:T(8,128)S(1)}) custom-call(f32[192,128]{1,0:T(8,128)S(1)} %collective-permute-done.12.w_o, f32[192,128]{1,0:T(8,128)S(1)} %collective-permute-done.13.w_e, f32[128,128]{1,0:T(8,128)S(1)} %get-tuple-element.73.w, f32[4,64,64]{2,1,0:T(8,128)S(1)} %copy-done.1, ...), custom_call_target="tpu_custom_call", output_to_operand_aliasing={{0}: (8, {})} | custom-call | tf_op jit(solution)/shard_map/coarse_kernel/pallas_call | solution.py:189
  69.8 0.0 collective-permute-done.8.m_o
  69.8 0.0 collective-permute-done.9.m_e
  69.8 0.0 copy-start.3
  69.8 2.9 %second_up_kernel.1 = (f32[1024,128]{1,0:T(8,128)S(1)}, f32[1024,128]{1,0:T(8,128)S(1)}) custom-call(f32[256,128]{1,0:T(8,128)S(1)} %collective-permute-done.8.m_o, f32[256,128]{1,0:T(8,128)S(1)} %collective-permute-done.9.m_e, f32[4,64,64]{2,1,0:T(8,128)S(1)} %copy-done.1, f32[64,64]{1,0:T(8,128)S(1)} %copy-done.7, ...), custom_call_target="tpu_custom_call", output_to_operand_aliasing={{0}: (8, {})} | custom-call | tf_op jit(solution)/shard_map/second_up_kernel/pallas_call | solution.py:189
  72.7 0.0 collective-permute-done.2.r_o
  72.8 0.0 collective-permute-done.3.r_e
  72.8 0.0 copy-done.3
  72.8 9.2 %last_kernel.1 = (f32[1280,256]{1,0:T(8,128)S(1)}, f32[1280,256]{1,0:T(8,128)S(1)}, f32[1280,256]{1,0:T(8,128)S(1)}, f32[1024,256]{1,0:T(8,128)}, f32[1024,256]{1,0:T(8,128)}) custom-call(f32[1024,256]{1,0:T(8,128)S(1)} %bitcast.6, f32[128,256]{1,0:T(8,128)S(1)} %collective-permute-done.2.r_o, ...), custom_call_target="tpu_custom_call", output_to_operand_aliasing={{0}: (9, {}), {1}: (10, {}), {2}: (11, {})} | custom-call | tf_op jit(solution)/shard_map/last_kernel/pallas_call | solution.py:189
Async XLA Ops:
  0.6 0.9 %copy-start = (f32[4,64,64]{2,1,0:T(8,128)S(1)}, f32[4,64,64]{2,1,0:T(8,128)}, u32[]{:S(2)}) copy-start(f32[4,64,64]{2,1,0:T(8,128)} %c.15) | copy-start | bytes 196612
  1.5 1.2 %copy-start.2 = (f32[64,16,256]{2,1,0:T(8,128)S(1)}, f32[64,16,256]{2,1,0:T(8,128)}, u32[]{:S(2)}) copy-start(f32[64,16,256]{2,1,0:T(8,128)} %param.5) | copy-start | bytes 3145732
  2.8 1.2 %copy-start.4 = (f32[64,16,256]{2,1,0:T(8,128)S(1)}, f32[64,16,256]{2,1,0:T(8,128)}, u32[]{:S(2)}) copy-start(f32[64,16,256]{2,1,0:T(8,128)} %param.6) | copy-start | bytes 3145732
  4.0 1.2 %copy-start.5 = (f32[64,16,256]{2,1,0:T(8,128)S(1)}, f32[64,16,256]{2,1,0:T(8,128)}, u32[]{:S(2)}) copy-start(f32[64,16,256]{2,1,0:T(8,128)} %param.7) | copy-start | bytes 3145732
  5.2 0.8 copy-start.6
  9.3 13.2 %collective-permute-start = (f32[256,256]{1,0:T(8,128)S(1)}, f32[256,256]{1,0:T(8,128)S(1)}, u32[]{:S(2)}, u32[]{:S(2)}) collective-permute-start(f32[256,256]{1,0:T(8,128)S(1)} %get-tuple-element.46.e_o), channel_id=1, source_target_pairs={{0,31},{1,2},{2,1},{3,4},{4,3},{5,6},{6,5},{7,8},{8,7},{9,10},{10,... | collective-permute-start | bytes 786440 | tf_op jit(solution)/shard_map/edge/ppermute | solution.py:218
  15.8 17.4 %collective-permute-start.1 = (f32[256,256]{1,0:T(8,128)S(1)}, f32[256,256]{1,0:T(8,128)S(1)}, u32[]{:S(2)}, u32[]{:S(2)}) collective-permute-start(f32[256,256]{1,0:T(8,128)S(1)} %get-tuple-element.47.e_e), channel_id=1, source_target_pairs={{0,1},{1,0},{2,3},{3,2},{4,5},{5,4},{6,7},{7,6},{8,9},{9,8},{10,11... | collective-permute-start | bytes 786440 | tf_op jit(solution)/shard_map/edge/ppermute | solution.py:218
  17.0 17.9 %collective-permute-start.4 = (f32[448,128]{1,0:T(8,128)S(1)}, f32[448,128]{1,0:T(8,128)S(1)}, u32[]{:S(2)}, u32[]{:S(2)}) collective-permute-start(f32[448,128]{1,0:T(8,128)S(1)} %get-tuple-element.60), channel_id=1, source_target_pairs={{0,31},{1,2},{2,1},{3,4},{4,3},{5,6},{6,5},{7,8},{8,7},{9,10},{10,... | collective-permute-start | bytes 688136 | tf_op jit(solution)/shard_map/stiff/ppermute | solution.py:218
  18.3 19.7 %collective-permute-start.5 = (f32[448,128]{1,0:T(8,128)S(1)}, f32[448,128]{1,0:T(8,128)S(1)}, u32[]{:S(2)}, u32[]{:S(2)}) collective-permute-start(f32[448,128]{1,0:T(8,128)S(1)} %get-tuple-element.61), channel_id=1, source_target_pairs={{0,1},{1,0},{2,3},{3,2},{4,5},{5,4},{6,7},{7,6},{8,9},{9,8},{10,11... | collective-permute-start | bytes 688136 | tf_op jit(solution)/shard_map/stiff/ppermute | solution.py:218
  19.0 14.2 %copy-start.1 = (f32[4,64,64]{2,1,0:T(8,128)S(1)}, f32[4,64,64]{2,1,0:T(8,128)}, u32[]{:S(2)}) copy-start(f32[4,64,64]{2,1,0:T(8,128)} %c.15) | copy-start | bytes 196612
  34.5 7.6 %collective-permute-start.6 = (f32[128,128]{1,0:T(8,128)S(1)}, f32[128,128]{1,0:T(8,128)S(1)}, u32[]{:S(2)}, u32[]{:S(2)}) collective-permute-start(f32[128,128]{1,0:T(8,128)S(1)} %get-tuple-element.62), channel_id=1, source_target_pairs={{0,31},{1,2},{2,1},{3,4},{4,3},{5,6},{6,5},{7,8},{8,7},{9,10},{10,... | collective-permute-start | bytes 196616 | tf_op jit(solution)/shard_map/second/ppermute | solution.py:218
  34.9 7.2 %collective-permute-start.7 = (f32[128,128]{1,0:T(8,128)S(1)}, f32[128,128]{1,0:T(8,128)S(1)}, u32[]{:S(2)}, u32[]{:S(2)}) collective-permute-start(f32[128,128]{1,0:T(8,128)S(1)} %get-tuple-element.63), channel_id=1, source_target_pairs={{0,1},{1,0},{2,3},{3,2},{4,5},{5,4},{6,7},{7,6},{8,9},{9,8},{10,11... | collective-permute-start | bytes 196616 | tf_op jit(solution)/shard_map/second/ppermute | solution.py:218
  42.1 23.7 %copy-start.7 = (f32[64,64]{1,0:T(8,128)S(1)}, f32[64,64]{1,0:T(8,128)}, u32[]{:S(2)}) copy-start(f32[64,64]{1,0:T(8,128)} %v.7) | copy-start | bytes 49156
  43.6 4.3 %collective-permute-start.11 = (f32[128,128]{1,0:T(8,128)S(1)}, f32[128,128]{1,0:T(8,128)S(1)}, u32[]{:S(2)}, u32[]{:S(2)}) collective-permute-start(f32[128,128]{1,0:T(8,128)S(1)} %get-tuple-element.69), channel_id=1, source_target_pairs={{0,1},{1,0},{2,3},{3,2},{4,5},{5,4},{6,7},{7,6},{8,9},{9,8},{10,11... | collective-permute-start | bytes 196616 | tf_op jit(solution)/shard_map/third/ppermute | solution.py:218
  43.7 7.9 %collective-permute-start.10 = (f32[128,128]{1,0:T(8,128)S(1)}, f32[128,128]{1,0:T(8,128)S(1)}, u32[]{:S(2)}, u32[]{:S(2)}) collective-permute-start(f32[128,128]{1,0:T(8,128)S(1)} %get-tuple-element.69), channel_id=1, source_target_pairs={{0,31},{1,2},{2,1},{3,4},{4,3},{5,6},{6,5},{7,8},{8,7},{9,10},{10,... | collective-permute-start | bytes 196616 | tf_op jit(solution)/shard_map/third/ppermute | solution.py:218
  53.3 7.9 %collective-permute-start.12 = (f32[192,128]{1,0:T(8,128)S(1)}, f32[192,128]{1,0:T(8,128)S(1)}, u32[]{:S(2)}, u32[]{:S(2)}) collective-permute-start(f32[192,128]{1,0:T(8,128)S(1)} %get-tuple-element.71), channel_id=1, source_target_pairs={{0,30},{1,31},{2,4},{3,5},{4,2},{5,3},{6,8},{7,9},{8,6},{9,7},{10,... | collective-permute-start | bytes 294920 | tf_op jit(solution)/shard_map/coarse/ppermute | solution.py:218
  53.4 16.4 %collective-permute-start.8 = (f32[256,128]{1,0:T(8,128)S(1)}, f32[256,128]{1,0:T(8,128)S(1)}, u32[]{:S(2)}, u32[]{:S(2)}) collective-permute-start(f32[256,128]{1,0:T(8,128)S(1)} %get-tuple-element.67), channel_id=1, source_target_pairs={{0,31},{1,2},{2,1},{3,4},{4,3},{5,6},{6,5},{7,8},{8,7},{9,10},{10,... | collective-permute-start | bytes 393224 | tf_op jit(solution)/shard_map/res1/ppermute | solution.py:218
  56.5 13.3 %collective-permute-start.9 = (f32[256,128]{1,0:T(8,128)S(1)}, f32[256,128]{1,0:T(8,128)S(1)}, u32[]{:S(2)}, u32[]{:S(2)}) collective-permute-start(f32[256,128]{1,0:T(8,128)S(1)} %get-tuple-element.68), channel_id=1, source_target_pairs={{0,1},{1,0},{2,3},{3,2},{4,5},{5,4},{6,7},{7,6},{8,9},{9,8},{10,11... | collective-permute-start | bytes 393224 | tf_op jit(solution)/shard_map/res1/ppermute | solution.py:218
  56.5 16.2 %collective-permute-start.2 = (f32[128,256]{1,0:T(8,128)S(1)}, f32[128,256]{1,0:T(8,128)S(1)}, u32[]{:S(2)}, u32[]{:S(2)}) collective-permute-start(f32[128,256]{1,0:T(8,128)S(1)} %get-tuple-element.58), channel_id=1, source_target_pairs={{0,31},{1,2},{2,1},{3,4},{4,3},{5,6},{6,5},{7,8},{8,7},{9,10},{10,... | collective-permute-start | bytes 393224 | tf_op jit(solution)/shard_map/res0/ppermute | solution.py:218
  59.0 13.7 %collective-permute-start.3 = (f32[128,256]{1,0:T(8,128)S(1)}, f32[128,256]{1,0:T(8,128)S(1)}, u32[]{:S(2)}, u32[]{:S(2)}) collective-permute-start(f32[128,256]{1,0:T(8,128)S(1)} %get-tuple-element.59), channel_id=1, source_target_pairs={{0,1},{1,0},{2,3},{3,2},{4,5},{5,4},{6,7},{7,6},{8,9},{9,8},{10,11... | collective-permute-start | bytes 393224 | tf_op jit(solution)/shard_map/res0/ppermute | solution.py:218
  61.2 4.6 %collective-permute-start.13 = (f32[192,128]{1,0:T(8,128)S(1)}, f32[192,128]{1,0:T(8,128)S(1)}, u32[]{:S(2)}, u32[]{:S(2)}) collective-permute-start(f32[192,128]{1,0:T(8,128)S(1)} %get-tuple-element.72), channel_id=1, source_target_pairs={{0,2},{1,3},{2,0},{3,1},{4,6},{5,7},{6,4},{7,5},{8,10},{9,11},{10,... | collective-permute-start | bytes 294920 | tf_op jit(solution)/shard_map/coarse/ppermute | solution.py:218
  69.8 3.0 %copy-start.3 = (f32[64,16,256]{2,1,0:T(8,128)S(1)}, f32[64,16,256]{2,1,0:T(8,128)}, u32[]{:S(2)}) copy-start(f32[64,16,256]{2,1,0:T(8,128)} %param.5) | copy-start | bytes 3145732
